TPU v7x, 128 devices: a whole 4x4x4 slice. The times are simulated.
128 devices in a mesh: ty: 8 (over z, core), tx: 16 (over y, x).
Axes of the slice: x: 4, y: 4, z: 4, core: 2. Of those that a mesh axis runs over, the one named last changes fastest.
Arguments:
- strips: bfloat16 [2, 8, 16, 4, 8, 128, 128], P(None, 'ty', 'tx'), may hold values from -6 to 6
- centers: bfloat16 [2, 8, 16, 8, 128, 128], P(None, 'ty', 'tx'), may hold values from -6 to 6
- match_lists: int32 [2, 8, 16, 5, 8, 2], P(None, 'ty', 'tx'), may hold values from 0 to 1023, as said below
- match_counts: int32 [2, 8, 16, 5], P(None, 'ty', 'tx'), may hold values from 0 to 8, as said below
- spring_stiffness: float32 [2, 8, 16], P(None, 'ty', 'tx'), may hold values from 0.5 to 6
Outputs:
- vertex_shift: float32 [2, 2, 8, 16, 1024], P(None, None, 'ty', 'tx')
- match_shift: float32 [2, 2, 8, 16, 5, 8], P(None, None, 'ty', 'tx')
Inputs may be any that keep to these rules, and one draw needn't show every extreme that they name: `match_lists`: entry [s, r, c, k, j, 0] is a vertex of tile (r, c) of section s and entry [s, r, c, k, j, 1] a vertex of its partner tile in direction k. The lists are mirrored: slot j of the east list of tile (r, c) equals slot j of the west list of tile (r, c+1) with its two vertices swapped; likewise south and north lists, and the cross lists of the two sections. `match_counts`: slots j below the count are matches, the others are unused. Counts are mirrored like the lists, and are 0 in directions that leave the slab.
All inputs are finite; a program needn't handle non-finite values.
Results may differ from a plain program's by a relative error of at most 0.0003.
Values may be sent and summed in bfloat16 or wider, within the bound.
No kernel may reach another device: no remote copies, remote signals or barrier semaphores. Data moves between devices by JAX's collectives and lax.ppermute only.
A program may use at most 128 MiB of HBM per device.

v0:
```python
import jax
import jax.numpy as jnp
from jax import lax
from jax.sharding import PartitionSpec as P

P_SIZE = 8
W = 128
V = 32
ITERS = 3


precise = lax.Precision.HIGHEST
anchor_weight = 0.05
epsilon = 1e-06


def with_halo(block, sides, width):
    for axis, dim in sides:
        count = lax.axis_size(axis)
        forward = [(i, i + 1) for i in range(count - 1)]
        backward = [(target, source) for source, target in forward]
        low = lax.ppermute(
            lax.slice_in_dim(block, block.shape[dim] - width, None, axis=dim), axis, forward
        )
        high = lax.ppermute(lax.slice_in_dim(block, 0, width, axis=dim), axis, backward)
        block = jnp.concatenate([low, block, high], axis=dim)
    return block


def fourier_tables():
    indices = jnp.arange(W, dtype=jnp.int32)
    phases = indices[:, None] * indices[None, :] % W
    angles = phases.astype(jnp.float32) * (2.0 * jnp.pi / W)
    return (jnp.cos(angles), jnp.sin(angles))


def spectrum(pixels, tables):
    cos_table, sin_table = tables
    values = pixels.astype(jnp.float32)
    by_cos = jnp.einsum("...mn,nv->...mv", values, cos_table, precision=precise)
    by_sin = jnp.einsum("...mn,nv->...mv", values, sin_table, precision=precise)
    real_part = jnp.einsum("um,...mv->...uv", cos_table, by_cos, precision=precise) - jnp.einsum(
        "um,...mv->...uv", sin_table, by_sin, precision=precise
    )
    imag_part = -(
        jnp.einsum("um,...mv->...uv", cos_table, by_sin, precision=precise)
        + jnp.einsum("um,...mv->...uv", sin_table, by_cos, precision=precise)
    )
    return (real_part, imag_part)


def lag_values():
    indices = jnp.arange(W, dtype=jnp.int32)
    midpoint = W // 2
    lagged = jnp.where(indices < midpoint, indices, jnp.where(indices == midpoint, 0, indices - W))
    return lagged.astype(jnp.float32)


def displacement(own_spec, partner_spec, tables):
    cos_table, sin_table = tables
    cross_real = own_spec[0] * partner_spec[0] + own_spec[1] * partner_spec[1]
    cross_imag = own_spec[1] * partner_spec[0] - own_spec[0] * partner_spec[1]
    left_part = jnp.einsum(
        "...uv,vq->...uq", cross_real, cos_table, precision=precise
    ) - jnp.einsum("...uv,vq->...uq", cross_imag, sin_table, precision=precise)
    right_part = jnp.einsum(
        "...uv,vq->...uq", cross_real, sin_table, precision=precise
    ) + jnp.einsum("...uv,vq->...uq", cross_imag, cos_table, precision=precise)
    surface = jnp.einsum("pu,...uq->...pq", cos_table, left_part, precision=precise) - jnp.einsum(
        "pu,...uq->...pq", sin_table, right_part, precision=precise
    )
    surface = surface / float(W * W * W)
    squared = surface * surface
    weight = squared * squared
    totals = jnp.sum(weight, axis=(-2, -1)) + epsilon
    lagged = lag_values()
    toward_rows = jnp.sum(weight * lagged[:, None], axis=(-2, -1))
    toward_cols = jnp.sum(weight * lagged[None, :], axis=(-2, -1))
    return jnp.stack([toward_rows / totals, toward_cols / totals]) * (2.0 / W)


def join_border(interior, border, along):
    return tuple(
        (
            jnp.concatenate([inner_part, jnp.expand_dims(outer_part, along)], axis=along)
            for inner_part, outer_part in zip(interior, border)
        )
    )


def neighbour_sum(vector):
    column = jnp.arange(V * V, dtype=jnp.int32) % V
    single = jnp.zeros(vector.shape[:-1] + (1,), vector.dtype)
    row_zeros = jnp.zeros(vector.shape[:-1] + (V,), vector.dtype)
    from_left = jnp.concatenate([single, vector[..., :-1]], axis=-1) * (column > 0).astype(
        vector.dtype
    )
    from_right = jnp.concatenate([vector[..., 1:], single], axis=-1) * (column < V - 1).astype(
        vector.dtype
    )
    from_above = jnp.concatenate([row_zeros, vector[..., :-V]], axis=-1)
    from_below = jnp.concatenate([vector[..., V:], row_zeros], axis=-1)
    return from_left + from_right + from_above + from_below


def local(strips, centers, match_lists, match_counts, spring_stiffness):
    tables = fourier_tables()
    east_spec = spectrum(strips[:, :, :, 0], tables)
    south_spec = spectrum(strips[:, :, :, 2], tables)
    west_inner = spectrum(strips[:, :, 1:, 1], tables)
    north_inner = spectrum(strips[:, 1:, :, 3], tables)
    rim_cols = with_halo(jnp.stack([strips[:, :, 0, 1], strips[:, :, -1, 0]]), (("tx", 0),), 1)
    rim_rows = with_halo(jnp.stack([strips[:, 0, :, 3], strips[:, -1, :, 2]]), (("ty", 0),), 1)
    shift_east = displacement(
        east_spec, join_border(west_inner, spectrum(rim_cols[3], tables), 2), tables
    )
    shift_south = displacement(
        south_spec, join_border(north_inner, spectrum(rim_rows[3], tables), 1), tables
    )
    edge_west = displacement(
        spectrum(strips[:, :, 0, 1], tables), spectrum(rim_cols[0], tables), tables
    )
    edge_north = displacement(
        spectrum(strips[:, 0, :, 3], tables), spectrum(rim_rows[0], tables), tables
    )
    shift_west = jnp.concatenate([edge_west[:, :, :, None], -shift_east[:, :, :, :-1]], axis=3)
    shift_north = jnp.concatenate([edge_north[:, :, None], -shift_south[:, :, :-1]], axis=2)
    center_spec = spectrum(centers, tables)
    cross = displacement(
        (center_spec[0][0], center_spec[1][0]), (center_spec[0][1], center_spec[1][1]), tables
    )
    shift_cross = jnp.stack([cross, -cross], axis=1)
    match_shift = jnp.stack([shift_east, shift_west, shift_south, shift_north, shift_cross], axis=4)
    valid = (jnp.arange(P_SIZE, dtype=jnp.int32) < match_counts[..., None]).astype(jnp.float32)
    vertex_ids = jnp.arange(V * V, dtype=jnp.int32)
    own_table = (match_lists[..., 0, None] == vertex_ids).astype(jnp.float32) * valid[..., None]
    partner_table = (match_lists[..., 1, None] == vertex_ids).astype(jnp.float32)
    stiffness = spring_stiffness[..., None]
    degree = neighbour_sum(jnp.ones((V * V,), jnp.float32))
    diagonal = anchor_weight + stiffness * degree + jnp.sum(own_table, axis=(3, 4))
    rhs_values = jnp.einsum("strkjv,cstrkj->cstrv", own_table, match_shift, precision=precise)
    solution = jnp.zeros_like(rhs_values)
    residual = rhs_values
    precond = residual / diagonal

    def global_norm(current, scaled):
        return lax.psum(jnp.sum(current * scaled), ("ty", "tx"))

    direction = precond
    norm_now = global_norm(residual, precond)
    for iteration in range(ITERS):
        own_values = jnp.einsum("strkjv,cstrv->cstrkj", own_table, direction, precision=precise)
        padded = with_halo(direction, (("ty", 2), ("tx", 3)), 1)
        beside = [
            padded[:, :, 1:-1, 2:],
            padded[:, :, 1:-1, :-2],
            padded[:, :, 2:, 1:-1],
            padded[:, :, :-2, 1:-1],
            direction[:, ::-1],
        ]
        partner_values = jnp.stack(
            [
                jnp.einsum(
                    "strjv,cstrv->cstrj",
                    partner_table[:, :, :, number],
                    beside[number],
                    precision=precise,
                )
                for number in range(5)
            ],
            axis=4,
        )
        coupling = jnp.einsum(
            "strkjv,cstrkj->cstrv", own_table, own_values - partner_values, precision=precise
        )
        product = (
            anchor_weight * direction
            + stiffness * (degree * direction - neighbour_sum(direction))
            + coupling
        )
        step_size = norm_now / lax.psum(jnp.sum(direction * product), ("ty", "tx"))
        solution = solution + step_size * direction
        residual = residual - step_size * product
        precond = residual / diagonal
        norm_next = global_norm(residual, precond)
        direction = precond + norm_next / norm_now * direction
        norm_now = norm_next
    return (solution, match_shift)


def solution(mesh):
    return jax.shard_map(
        local,
        mesh=mesh,
        in_specs=(
            P(None, "ty", "tx", None, None, None, None),
            P(None, "ty", "tx", None, None, None),
            P(None, "ty", "tx", None, None, None),
            P(None, "ty", "tx", None),
            P(None, "ty", "tx"),
        ),
        out_specs=(P(None, None, "ty", "tx", None), P(None, None, "ty", "tx", None, None)),
        check_vma=False,
    )
```

profile of v0, /device:TPU:1, one launch (start us, length us, event | category | flops | bytes accessed | tf_op | source)
XLA Modules:
  0.0 535.0 jit_solution(1878026352332238762)
XLA Ops:
  0.6 3.0 slice_bitcast_fusion.3
  3.6 4.7 collective-permute-start.1
  8.4 4.4 collective-permute-start.3
  14.0 1.9 collective-permute-start.2
  35.6 2.2 fusion.243
  37.8 2.2 convolution_add_fusion.9
  40.0 2.2 fusion.215
  42.2 2.4 fusion.219
  45.8 2.3 fusion.255
  48.1 2.2 fusion.28
  51.5 2.2 fusion.231
  53.8 2.2 fusion.14
  56.2 1.7 fusion.102
  59.4 2.8 convolution_add_fusion.3
  62.2 1.9 convolution_bitcast_fusion.10
  64.1 1.5 fusion.237
  65.6 1.9 convolution_bitcast_fusion.11
  71.9 1.5 multiply_subtract_fusion.2
  73.3 1.3 fusion.75
  74.7 1.3 fusion.73
  76.0 1.9 convolution_bitcast_fusion.2
  79.2 1.9 convolution_bitcast_fusion.3
  81.1 1.6 fusion.217
  85.2 1.5 multiply_subtract_fusion
  86.7 1.3 fusion.63
  89.4 1.9 convolution_bitcast_fusion.15
  92.5 1.9 convolution_bitcast_fusion.14
  98.6 1.4 multiply_subtract_fusion.3
  101.4 1.3 fusion.81
  102.8 1.9 convolution_bitcast_fusion.6
  105.9 1.9 convolution_bitcast_fusion.7
  109.0 1.5 fusion.12
  112.0 1.4 multiply_subtract_fusion.1
  114.8 1.3 fusion.69
  116.1 1.3 convolution_subtract_fusion.10
  118.7 1.3 convolution_add_fusion.7
  120.1 1.3 convolution_subtract_fusion.2
  122.6 1.7 convolution_add_fusion.1
  124.4 1.3 convolution_add_fusion.10
  125.7 1.3 convolution_subtract_fusion.14
  128.3 1.3 convolution_add_fusion.4
  129.7 1.3 convolution_subtract_fusion.6
  134.7 1.9 multiply_reduce_fusion.3
  136.6 1.7 multiply_reduce_fusion.1
  138.9 3.6 collective-permute-start.4
  142.5 1.9 collective-permute-start.5
  144.5 3.0 collective-permute-done.5
  149.0 4.6 collective-permute-start.7
  155.5 2.0 fusion.54
  158.6 69.9 %all-reduce.12 = (f32[]{:T(128)}, f32[]{:T(128)}) all-reduce(f32[]{:T(128)} %get-tuple-element.21, f32[]{:T(128)} %get-tuple-element.20), channel_id=1, replica_groups=mesh['ty'=8,'tx'=16] {'ty','tx'}, use_global_device_ids=true, to_apply=%region_17.18 | all-reduce | flops 2 | bytes 16 | tf_op jit(solution)/shard_map/psum | solution.py:147
  230.5 62.8 %psum.44 = f32[]{:T(128)} all-reduce(f32[]{:T(128)} %get-tuple-element.32), channel_id=1, replica_groups=mesh['ty'=8,'tx'=16] {'ty','tx'}, use_global_device_ids=true, to_apply=%region_21.22 | all-reduce | flops 1 | bytes 8 | tf_op jit(solution)/shard_map/psum | solution.py:147
  294.7 3.5 collective-permute-start.8
  298.2 1.9 collective-permute-start.9
  300.2 3.0 collective-permute-done.9
  304.7 4.0 collective-permute-start.11
  310.6 2.0 fusion.56
  313.7 66.6 %psum.45 = f32[]{:T(128)} all-reduce(f32[]{:T(128)} %get-tuple-element.78), channel_id=1, replica_groups=mesh['ty'=8,'tx'=16] {'ty','tx'}, use_global_device_ids=true, to_apply=%region_23.24 | all-reduce | flops 1 | bytes 8 | tf_op jit(solution)/shard_map/psum | solution.py:181
  382.2 63.0 %psum.46 = f32[]{:T(128)} all-reduce(f32[]{:T(128)} %get-tuple-element.30), channel_id=1, replica_groups=mesh['ty'=8,'tx'=16] {'ty','tx'}, use_global_device_ids=true, to_apply=%region_25.26 | all-reduce | flops 1 | bytes 8 | tf_op jit(solution)/shard_map/psum | solution.py:147
  446.5 3.3 collective-permute-start.12
  449.8 1.9 collective-permute-start.13
  451.8 3.0 collective-permute-done.13
  456.3 4.0 collective-permute-start.15
  462.2 2.0 fusion.58
  465.9 66.8 %psum.47 = f32[]{:T(128)} all-reduce(f32[]{:T(128)} %fusion.90), channel_id=1, replica_groups=mesh['ty'=8,'tx'=16] {'ty','tx'}, use_global_device_ids=true, to_apply=%region_27.28 | all-reduce | flops 1 | bytes 8 | tf_op jit(solution)/shard_map/psum | solution.py:181
  (160 shorter events, 69.7 us)
Async XLA Ops:
  0.6 15.3 %copy-start = (bf16[2,1,1,8,128,128]{5,4,3,2,1,0:T(8,128)(2,1)S(1)}, bf16[2,1,1,8,128,128]{5,4,3,2,1,0:T(8,128)(2,1)}, u32[]{:S(2)}) copy-start(bf16[2,1,1,8,128,128]{5,4,3,2,1,0:T(8,128)(2,1)} %param.6) | copy-start | bytes 1572868
  3.6 58.6 %collective-permute-start.1 = (bf16[1,2,1,8,128,128]{5,4,3,1,2,0:T(8,128)(2,1)}, bf16[1,2,1,8,128,128]{5,4,3,1,2,0:T(8,128)(2,1)}, u32[]{:S(2)}, u32[]{:S(2)}) collective-permute-start(bf16[1,2,1,8,128,128]{5,4,3,1,2,0:T(8,128)(2,1)} %get-tuple-element.46), channel_id=1, source_target_pairs={{0,1},{1,2},{2,3},{3,4},{4,5},{5,6},{6,7},{7,8},{8,9},{9,10},{10,1... | collective-permute-start | bytes 1572872 | tf_op jit(solution)/shard_map/ppermute | solution.py:22
  8.4 67.7 %collective-permute-start.3 = (bf16[1,2,1,8,128,128]{5,4,3,1,2,0:T(8,128)(2,1)}, bf16[1,2,1,8,128,128]{5,4,3,1,2,0:T(8,128)(2,1)}, u32[]{:S(2)}, u32[]{:S(2)}) collective-permute-start(bf16[1,2,1,8,128,128]{5,4,3,1,2,0:T(8,128)(2,1)} %get-tuple-element.49), channel_id=1, source_target_pairs={{0,16},{16,32},{32,48},{48,64},{64,80},{80,96},{96,112},{1,17},{17... | collective-permute-start | bytes 1572872 | tf_op jit(solution)/shard_map/ppermute | solution.py:22
  12.7 76.6 %collective-permute-start = (bf16[1,2,1,8,128,128]{5,4,3,1,2,0:T(8,128)(2,1)}, bf16[1,2,1,8,128,128]{5,4,3,1,2,0:T(8,128)(2,1)}, u32[]{:S(2)}, u32[]{:S(2)}) collective-permute-start(bf16[1,2,1,8,128,128]{5,4,3,1,2,0:T(8,128)(2,1)} %get-tuple-element.47), channel_id=1, source_target_pairs={{1,0},{2,1},{3,2},{4,3},{5,4},{6,5},{7,6},{8,7},{9,8},{10,9},{11,1... | collective-permute-start | bytes 1572872 | tf_op jit(solution)/shard_map/ppermute | solution.py:25
  14.0 88.7 %collective-permute-start.2 = (bf16[1,2,1,8,128,128]{5,4,3,1,2,0:T(8,128)(2,1)}, bf16[1,2,1,8,128,128]{5,4,3,1,2,0:T(8,128)(2,1)}, u32[]{:S(2)}, u32[]{:S(2)}) collective-permute-start(bf16[1,2,1,8,128,128]{5,4,3,1,2,0:T(8,128)(2,1)} %get-tuple-element.48), channel_id=1, source_target_pairs={{16,0},{32,16},{48,32},{64,48},{80,64},{96,80},{112,96},{17,1},{33... | collective-permute-start | bytes 1572872 | tf_op jit(solution)/shard_map/ppermute | solution.py:25
  22.6 1.9 copy-start.2
  25.4 8.9 %copy-start.3 = (f32[2,8,128,128]{2,3,1,0:T(8,128)}, f32[2,8,128,128]{2,3,1,0:T(8,128)S(1)}, u32[]{:S(2)}) copy-start(f32[2,8,128,128]{2,3,1,0:T(8,128)S(1)} %convolution_bitcast_fusion.12) | copy-start | bytes 3145732
  28.0 14.2 %copy-start.5 = (f32[2,8,128,128]{2,3,1,0:T(8,128)}, f32[2,8,128,128]{2,3,1,0:T(8,128)S(1)}, u32[]{:S(2)}) copy-start(f32[2,8,128,128]{2,3,1,0:T(8,128)S(1)} %convolution_bitcast_fusion.5) | copy-start | bytes 3145732
  53.7 2.3 copy-start.13
  53.7 2.3 copy-start.17
  53.7 5.6 %copy-start.14 = (f32[1024]{0:T(1024)S(1)}, f32[1024]{0:T(1024)}, u32[]{:S(2)}) copy-start(f32[1024]{0:T(1024)} %constant.110.clone.1) | copy-start | bytes 12292
  53.7 5.6 %copy-start.15 = (f32[1024]{0:T(1024)S(1)}, f32[1024]{0:T(1024)}, u32[]{:S(2)}) copy-start(f32[1024]{0:T(1024)} %constant.111.clone.1) | copy-start | bytes 12292
  53.7 5.6 %copy-start.16 = (f32[1024]{0:T(1024)S(1)}, f32[1024]{0:T(1024)}, u32[]{:S(2)}) copy-start(f32[1024]{0:T(1024)} %constant.112.clone.1) | copy-start | bytes 12292
  53.7 5.6 %copy-start.18 = (f32[2,1,1]{0,2,1:T(1,128)S(1)}, f32[2,1,1]{0,2,1:T(1,128)}, u32[]{:S(2)}) copy-start(f32[2,1,1]{0,2,1:T(1,128)} %param.9) | copy-start | bytes 28
  70.0 1.3 copy-start.4
  70.0 1.5 copy-start.8
  70.0 1.8 copy-start.12
  83.9 1.3 copy-start.11
  97.1 1.3 copy-start.7
  97.1 1.5 copy-start.10
  110.5 1.3 copy-start.6
  110.5 1.5 copy-start.9
  138.9 5.7 %collective-permute-start.4 = (f32[2,2,1,1,1024]{4,0,1,3,2:T(2,128)S(1)}, f32[2,2,1,1,1024]{4,0,1,3,2:T(2,128)S(1)}, u32[]{:S(2)}, u32[]{:S(2)}) collective-permute-start(f32[2,2,1,1,1024]{4,0,1,3,2:T(2,128)S(1)} %get-tuple-element.75), channel_id=1, source_target_pairs={{0,16},{16,32},{32,48},{48,64},{64,80},{80,96},{96,112},{1,17},{17... | collective-permute-start | bytes 49160 | tf_op jit(solution)/shard_map/ppermute | solution.py:22
  142.5 5.1 collective-permute-start.5
  147.6 6.0 %collective-permute-start.6 = (f32[2,2,3,1,1024]{4,0,1,3,2:T(2,128)S(1)}, f32[2,2,3,1,1024]{4,0,1,3,2:T(2,128)S(1)}, u32[]{:S(2)}, u32[]{:S(2)}) collective-permute-start(f32[2,2,3,1,1024]{4,0,1,3,2:T(2,128)S(1)} %pad_maximum_fusion), channel_id=1, source_target_pairs={{1,0},{2,1},{3,2},{4,3},{5,4},{6,5},{7,6},{8,7},{9,8},{10,9},{11,1... | collective-permute-start | bytes 147464 | tf_op jit(solution)/shard_map/ppermute | solution.py:25
  149.0 5.8 %collective-permute-start.7 = (f32[2,2,3,1,1024]{4,0,1,3,2:T(2,128)S(1)}, f32[2,2,3,1,1024]{4,0,1,3,2:T(2,128)S(1)}, u32[]{:S(2)}, u32[]{:S(2)}) collective-permute-start(f32[2,2,3,1,1024]{4,0,1,3,2:T(2,128)S(1)} %pad_maximum_fusion), channel_id=1, source_target_pairs={{0,1},{1,2},{2,3},{3,4},{4,5},{5,6},{6,7},{7,8},{8,9},{9,10},{10,1... | collective-permute-start | bytes 147464 | tf_op jit(solution)/shard_map/ppermute | solution.py:22
  157.5 377.3 %copy-start.1 = (bf16[2,1,1,8,128,128]{5,4,3,2,1,0:T(8,128)(2,1)S(1)}, bf16[2,1,1,8,128,128]{5,4,3,2,1,0:T(8,128)(2,1)}, u32[]{:S(2)}) copy-start(bf16[2,1,1,8,128,128]{5,4,3,2,1,0:T(8,128)(2,1)} %param.6) | copy-start | bytes 1572868
  294.7 5.6 %collective-permute-start.8 = (f32[2,2,1,1,1024]{4,0,1,3,2:T(2,128)S(1)}, f32[2,2,1,1,1024]{4,0,1,3,2:T(2,128)S(1)}, u32[]{:S(2)}, u32[]{:S(2)}) collective-permute-start(f32[2,2,1,1,1024]{4,0,1,3,2:T(2,128)S(1)} %multiply_add_fusion.7), channel_id=1, source_target_pairs={{0,16},{16,32},{32,48},{48,64},{64,80},{80,96},{96,112},{1,17},{17... | collective-permute-start | bytes 49160 | tf_op jit(solution)/shard_map/ppermute | solution.py:22
  298.2 5.1 collective-permute-start.9
  303.3 5.4 %collective-permute-start.10 = (f32[2,2,3,1,1024]{4,0,1,3,2:T(2,128)S(1)}, f32[2,2,3,1,1024]{4,0,1,3,2:T(2,128)S(1)}, u32[]{:S(2)}, u32[]{:S(2)}) collective-permute-start(f32[2,2,3,1,1024]{4,0,1,3,2:T(2,128)S(1)} %pad_maximum_fusion.1), channel_id=1, source_target_pairs={{1,0},{2,1},{3,2},{4,3},{5,4},{6,5},{7,6},{8,7},{9,8},{10,9},{11,1... | collective-permute-start | bytes 147464 | tf_op jit(solution)/shard_map/ppermute | solution.py:25
  304.7 5.2 collective-permute-start.11
  446.5 5.3 collective-permute-start.12
  449.8 5.1 collective-permute-start.13
  454.9 5.4 %collective-permute-start.14 = (f32[2,2,3,1,1024]{4,0,1,3,2:T(2,128)S(1)}, f32[2,2,3,1,1024]{4,0,1,3,2:T(2,128)S(1)}, u32[]{:S(2)}, u32[]{:S(2)}) collective-permute-start(f32[2,2,3,1,1024]{4,0,1,3,2:T(2,128)S(1)} %pad_maximum_fusion.2), channel_id=1, source_target_pairs={{1,0},{2,1},{3,2},{4,3},{5,4},{6,5},{7,6},{8,7},{9,8},{10,9},{11,1... | collective-permute-start | bytes 147464 | tf_op jit(solution)/shard_map/ppermute | solution.py:25
  456.3 5.2 collective-permute-start.15
where the time goes:
time: 545 us; the launch traced here: 535 us
  blocking collectives  329 us (60%)
  matrix products  131 us (24%)
  starting transfers between devices  45 us (8%)
  waiting for transfers between devices  12.1 us (2%)
  between operations  8.9 us (2%)
  local copies, waits for them, and re-layouts  5.89 us (1%)
    psum x3, blocking collectives, global_norm(): return lax.psum(jnp.sum(current * scaled), ('ty', 'tx'))  196 us
    psum x2, blocking collectives, local(): step_size = norm_now / lax.psum(jnp.sum(direction * product), ('ty', 'tx'))  133 us
    ppermute x8, starting transfers between devices, with_halo(): lax.ppermute(lax.slice_in_dim(block, block.shape[dim] - width, None, axis...  32.2 us
    dot_general x9, matrix products, spectrum(): jnp.einsum('um,...mv->...uv', sin_table, by_cos, precision=precise)  15.9 us
    dot_general x9, matrix products, spectrum(): jnp.einsum('um,...mv->...uv', cos_table, by_cos, precision=precise)  15.6 us
    ppermute x8, starting transfers between devices, with_halo(): lax.ppermute(lax.slice_in_dim(block, 0, width, axis=dim), axis, backward)  12.9 us
    dot_general x9, matrix products, spectrum(): jnp.einsum('um,...mv->...uv', cos_table, by_sin, precision=precise)  12.2 us
    dot_general x9, matrix products, spectrum(): by_sin = jnp.einsum('...mn,nv->...mv', values, sin_table, precision=precise)  12.2 us
  transfers between devices with their start and end apart: 16, of which 6 were waited for; matrix products, arithmetic and copies ran while one was open for 16% of the time, Pallas kernels for 0%

commit v1 on v0

v1 whole, which is shorter than its diff:
```python
import functools

import jax
import jax.numpy as jnp
import numpy as np
from jax import lax
from jax.experimental import pallas as pl
from jax.experimental.pallas import tpu as pltpu
from jax.sharding import PartitionSpec as P

P_SIZE = 8
W = 128
V = 32
HALF = P_SIZE // 2
SLOTS = 5 * P_SIZE
U = 72

anchor_weight = 0.05
epsilon = 1e-06
f32 = jnp.float32
bf16 = jnp.bfloat16


def split_table(table):
    table = np.asarray(table, np.float32)
    high = table.astype(jnp.bfloat16)
    return high, (table - high.astype(np.float32)).astype(jnp.bfloat16)


def fourier_tables():
    idx = np.arange(W)
    angles = 2.0 * np.pi * ((idx[:, None] * idx[None, :]) % W) / W
    cos, sin = np.cos(angles), np.sin(angles)
    cos_h, cos_l = split_table(cos)
    sin_h, sin_l = split_table(sin)
    along_cols = np.concatenate(
        [np.concatenate([cos_h, sin_h], 1), np.concatenate([cos_l, sin_l], 1)], 0
    )
    half_cos, half_sin = np.zeros((U, W)), np.zeros((U, W))
    half_cos[: W // 2 + 1], half_sin[: W // 2 + 1] = cos[: W // 2 + 1], sin[: W // 2 + 1]
    along_rows = np.concatenate(
        [np.concatenate([half_cos, -half_sin], 1), np.concatenate([-half_sin, -half_cos], 1)], 0
    )
    along_rows = np.concatenate(split_table(along_rows), 0)
    back_cols = np.concatenate(
        [np.concatenate([cos, sin], 1), np.concatenate([-sin, cos], 1)], 0
    )
    back_cols = np.concatenate(split_table(back_cols), 0)
    back_rows = np.zeros((W, W))
    back_rows[:, 0] = 1.0
    back_rows[:, 1 : W // 2] = 2.0 * cos[:, 1 : W // 2]
    back_rows[:, W // 2] = cos[:, W // 2]
    back_rows[:, W // 2 + 1 :] = -2.0 * sin[:, 1 : W // 2]
    back_h, back_l = split_table(back_rows / float(W * W * W))
    back_rows = np.concatenate([back_h, back_h, back_l], 1)
    lag = np.where(idx < W // 2, idx, np.where(idx == W // 2, 0, idx - W)).astype(np.float32)
    lag_rows = np.broadcast_to(lag[:, None], (W, W)).copy()
    lag_cols = np.broadcast_to(lag[None, :], (P_SIZE, W)).copy()
    return along_cols, along_rows, back_cols, back_rows, lag_rows, lag_cols


def high_low(values):
    high = values.astype(bf16)
    return high, (values - high.astype(f32)).astype(bf16)


def dot(left, right):
    return jnp.dot(left, right, preferred_element_type=f32)


def correlate_two(own, partner, tables, high_ref, low_ref):
    along_cols, along_rows, back_cols, back_rows, lag_rows = tables
    spectra = []
    for side, patches in enumerate((own, partner)):
        for t, patch in enumerate(patches):
            high, low = high_low(dot(jnp.concatenate([patch, patch], 1), along_cols[...]))
            lanes = pl.ds(t * W, W)
            high_ref[side, 0:W, lanes] = high[:, :W]
            high_ref[side, W : 2 * W, lanes] = high[:, W:]
            low_ref[side, 0:W, lanes] = low[:, :W]
            low_ref[side, W : 2 * W, lanes] = low[:, W:]
        both = dot(along_rows[...], high_ref[side])
        spectra.append(
            both[: 2 * U] + both[2 * U :] + dot(along_rows[0 : 2 * U], low_ref[side])
        )
    own_re, own_im = spectra[0][:U], spectra[0][U:]
    par_re, par_im = spectra[1][:U], spectra[1][U:]
    cross_re = own_re * par_re + own_im * par_im
    cross_im = own_im * par_re - own_re * par_im
    cross = jnp.concatenate(
        [
            jnp.concatenate([cross_re[:, :W], cross_im[:, :W]], 1),
            jnp.concatenate([cross_re[:, W:], cross_im[:, W:]], 1),
        ],
        0,
    )
    high, low = high_low(cross)
    both = dot(jnp.concatenate([high, low], 0), back_cols[0 : 2 * W])
    partly = both[: 2 * U] + both[2 * U :] + dot(high, back_cols[2 * W : 4 * W])
    first = lax.broadcasted_iota(jnp.int32, (8, W), 0) == 0
    stacked = []
    for t in range(2):
        real, imag = partly[t * U : (t + 1) * U, :W], partly[t * U : (t + 1) * U, W:]
        top = jnp.where(first, real[W // 2 : W // 2 + 8], imag[0:8])
        stacked.append(jnp.concatenate([real[: W // 2], top, imag[8 : W // 2]], 0))
    high, low = high_low(jnp.concatenate(stacked, 1))
    surface = dot(back_rows[:, 0 : 2 * W], jnp.concatenate([high, low], 0)) + dot(
        back_rows[:, 2 * W : 3 * W], high
    )
    squared = surface * surface
    weight = squared * squared
    lagged = lag_rows[...]
    totals = jnp.sum(weight, axis=0, keepdims=True)
    rowwise = jnp.sum(weight * jnp.concatenate([lagged, lagged], 1), axis=0, keepdims=True)
    return totals, rowwise


def correlate_four(load_own, load_partner, tables, high_ref, low_ref, tot_ref, row_ref, base):
    for g in range(2):
        totals, rowwise = correlate_two(
            [load_own(2 * g), load_own(2 * g + 1)],
            [load_partner(2 * g), load_partner(2 * g + 1)],
            tables,
            high_ref.at[g],
            low_ref.at[g],
        )
        for t in range(2):
            tot_ref[pl.ds(base + 2 * g + t, 1), :] = totals[:, t * W : (t + 1) * W]
            row_ref[pl.ds(base + 2 * g + t, 1), :] = rowwise[:, t * W : (t + 1) * W]


def offsets_on_lanes(tot_ref, row_ref, lag_cols, targets):
    tot, row = tot_ref[...], row_ref[...]
    denominator = jnp.sum(tot, axis=1, keepdims=True) + epsilon
    toward_rows = jnp.sum(row, axis=1, keepdims=True)
    toward_cols = jnp.sum(tot * lag_cols[0:1, :], axis=1, keepdims=True)
    lane = lax.broadcasted_iota(jnp.int32, tot.shape, 1)
    rows = []
    for toward in (toward_rows, toward_cols):
        shift = toward / denominator * (2.0 / W)
        rows.append(
            jnp.sum(jnp.where(lane == targets, shift, 0.0), axis=0, keepdims=True)
        )
    return jnp.concatenate(rows + [jnp.zeros((6, W), f32)], 0)


def cross_kernel(own_ref, par_ref, t1, t2, t3, t4, t5, lag_cols, out_ref, high_ref, low_ref, tot_ref, row_ref):
    step = pl.program_id(0)
    correlate_four(
        lambda j: own_ref[0, 0, 0, j],
        lambda j: par_ref[0, 0, 0, j],
        (t1, t2, t3, t4, t5),
        high_ref,
        low_ref,
        tot_ref,
        row_ref,
        step * HALF,
    )

    @pl.when(step == 1)
    def _():
        targets = 4 * P_SIZE + lax.broadcasted_iota(jnp.int32, (P_SIZE, W), 0)
        offset = offsets_on_lanes(tot_ref, row_ref, lag_cols, targets)
        out_ref[...] = offset - pltpu.roll(offset, SLOTS, 1)


def edge_kernel(sides, own_ref, r0, r1, r2, r3, t1, t2, t3, t4, t5, lag_cols, out_ref, par_ref, high_ref, low_ref, tot_ref, row_ref):
    which, section = pl.program_id(0), pl.program_id(1)
    for number, ref in enumerate((r0, r1, r2, r3)):

        @pl.when(which == number)
        def _():
            par_ref[...] = ref[section]

    correlate_four(
        lambda j: own_ref[0, 0, 0, 0, j],
        lambda j: par_ref[j],
        (t1, t2, t3, t4, t5),
        high_ref,
        low_ref,
        tot_ref,
        row_ref,
        which * P_SIZE + section * HALF,
    )

    @pl.when((which == 3) & (section == 1))
    def _():
        pair = lax.broadcasted_iota(jnp.int32, (4 * P_SIZE, W), 0)
        start = jnp.zeros_like(pair)
        for number in range(4):
            side = sides[number]
            start = jnp.where(pair // P_SIZE == number, side * P_SIZE + (side % 2) * HALF, start)
        targets = start + (pair % P_SIZE) // HALF * SLOTS + pair % HALF
        out_ref[...] = offsets_on_lanes(tot_ref, row_ref, lag_cols, targets)


def corr_scratch(pairs):
    return [
        pltpu.VMEM((2, 2, 2 * W, 2 * W), bf16),
        pltpu.VMEM((2, 2, 2 * W, 2 * W), bf16),
        pltpu.VMEM((pairs, W), f32),
        pltpu.VMEM((pairs, W), f32),
    ]


def whole(array):
    return pl.BlockSpec(array.shape, lambda *_: (0,) * array.ndim)


def cross_offsets(centers, tables):
    return pl.pallas_call(
        cross_kernel,
        grid=(2,),
        in_specs=[
            pl.BlockSpec((1, 1, 1, HALF, W, W), lambda i: (0, 0, 0, i, 0, 0)),
            pl.BlockSpec((1, 1, 1, HALF, W, W), lambda i: (1, 0, 0, i, 0, 0)),
        ]
        + [whole(t) for t in tables],
        out_specs=pl.BlockSpec((8, W), lambda i: (0, 0)),
        out_shape=jax.ShapeDtypeStruct((8, W), f32),
        scratch_shapes=corr_scratch(P_SIZE),
        name="cross_corr",
    )(centers, centers, *tables)


def edge_offsets(sides, strips, received, tables):
    return pl.pallas_call(
        edge_kernel,
        grid_spec=pltpu.PrefetchScalarGridSpec(
            num_scalar_prefetch=1,
            grid=(4, 2),
            in_specs=[
                pl.BlockSpec(
                    (1, 1, 1, 1, HALF, W, W),
                    lambda i, s, sides: (s, 0, 0, sides[i], sides[i] % 2, 0, 0),
                )
            ]
            + [pl.BlockSpec(r.shape, lambda i, s, sides: (0, 0, 0, 0)) for r in received]
            + [pl.BlockSpec(t.shape, lambda i, s, sides: (0, 0)) for t in tables],
            out_specs=pl.BlockSpec((8, W), lambda i, s, sides: (0, 0)),
            scratch_shapes=[pltpu.VMEM((HALF, W, W), bf16)] + corr_scratch(4 * P_SIZE),
        ),
        out_shape=jax.ShapeDtypeStruct((8, W), f32),
        name="edge_corr",
    )(sides, strips, *received, *tables)


def three_terms(values):
    high = values.astype(bf16)
    rest = values - high.astype(f32)
    middle = rest.astype(bf16)
    return jnp.concatenate([high, middle, (rest - middle.astype(f32)).astype(bf16)], 0)


def slot_tables(slots):
    vertex = slots[0:1, :]
    hit = lax.broadcasted_iota(jnp.int32, (W, W), 0) == vertex % W
    row = lax.broadcasted_iota(jnp.int32, (32, W), 0)
    lane = lax.broadcasted_iota(jnp.int32, (32, W), 1)
    section = jnp.where(lane < SLOTS, 0, 1)
    inside = (row % 8 == vertex // W) & ((row // 8) % 2 == section) & (lane < 2 * SLOTS)
    return jnp.where(hit, 1.0, 0.0).astype(bf16), jnp.where(inside, 1.0, 0.0)


def gather(field, hit, inside):
    found = dot(three_terms(field), hit)
    found = (found[:32] + found[32:64] + found[64:]) * inside
    return (
        jnp.sum(found[:16], axis=0, keepdims=True),
        jnp.sum(found[16:], axis=0, keepdims=True),
    )


def scatter(values, hit, inside):
    spread = jnp.concatenate(
        [jnp.broadcast_to(values[0], (16, W)), jnp.broadcast_to(values[1], (16, W))], 0
    )
    placed = lax.dot_general(
        three_terms(spread * inside), hit, (((1,), (1,)), ((), ())), preferred_element_type=f32
    )
    return placed[:32] + placed[32:64] + placed[64:]


def neighbour_sum(field):
    row = lax.broadcasted_iota(jnp.int32, field.shape, 0) % 8
    lane = lax.broadcasted_iota(jnp.int32, field.shape, 1)
    total = jnp.where(lane % V > 0, pltpu.roll(field, 1, 1), 0.0)
    total = total + jnp.where(lane % V < V - 1, pltpu.roll(field, W - 1, 1), 0.0)
    above = pltpu.roll(field, V, 1)
    wrapped = jnp.where(row > 0, pltpu.roll(above, 1, 0), 0.0)
    total = total + jnp.where(lane >= V, above, wrapped)
    below = pltpu.roll(field, W - V, 1)
    wrapped = jnp.where(row < 7, pltpu.roll(below, field.shape[0] - 1, 0), 0.0)
    return total + jnp.where(lane < W - V, below, wrapped)


def stiffness_rows(stiffness):
    row = lax.broadcasted_iota(jnp.int32, (32, W), 0)
    return jnp.where((row // 8) % 2 == 0, stiffness[0], stiffness[1])


def sided(parity, messages):
    even_x, even_y = parity[0] == 0, parity[1] == 0
    p1, p2, p3, p4 = (m[0:2, :] for m in messages)
    east, west = jnp.where(even_x, p1, p2), jnp.where(even_x, p2, p1)
    south, north = jnp.where(even_y, p3, p4), jnp.where(even_y, p4, p3)
    return east, west, south, north


def lane_kinds(shape):
    lane = lax.broadcasted_iota(jnp.int32, shape, 1)
    within = jnp.where(lane < SLOTS, lane, lane - SLOTS)
    return lane, within // P_SIZE, within % P_SIZE


def to_partner(sides):
    east, west, south, north = sides
    _, kind, _ = lane_kinds((2, W))
    low = jnp.where(kind == 0, pltpu.roll(east, W - P_SIZE, 1), pltpu.roll(south, W - P_SIZE, 1))
    high = jnp.where(kind == 1, pltpu.roll(west, P_SIZE, 1), pltpu.roll(north, P_SIZE, 1))
    return jnp.where((kind == 0) | (kind == 2), low, high)


def partner_values(own, sides):
    lane, kind, _ = lane_kinds((2, W))
    crossed = jnp.where(
        lane < SLOTS, pltpu.roll(own, W - SLOTS, 1), pltpu.roll(own, SLOTS, 1)
    )
    return jnp.where(kind == 4, crossed, to_partner(sides))


def padded(rows):
    return jnp.concatenate([rows, jnp.zeros((6, W), f32)], 0)


def start_kernel(parity, stiffness, slots, valid, cross, edge, m1, m2, m3, m4, field_ref, vals_ref, shift_ref, inv_ref):
    _, kind, slot = lane_kinds((2, W))
    mirrored = to_partner(sided(parity, (m1, m2, m3, m4)))
    here = ((kind == 0) | (kind == 2)) == (slot < HALF)
    shift = jnp.where(kind == 4, cross[0:2, :], jnp.where(here, edge[0:2, :], -mirrored))
    shift_ref[...] = padded(shift)
    hit, inside = slot_tables(slots)
    live = valid[0:1, :]
    ones = jnp.ones((32, W), f32)
    counts = scatter((live, live), hit, inside)
    diagonal = anchor_weight + stiffness_rows(stiffness) * neighbour_sum(ones) + counts
    inverse = 1.0 / diagonal
    rhs = scatter((live * shift[0:1], live * shift[1:2]), hit, inside)
    field = rhs / diagonal
    field_ref[...] = field
    inv_ref[...] = inverse
    vals_ref[...] = padded(jnp.concatenate(gather(field, hit, inside), 0))


def advance(parity, stiffness, slots, valid, field, vals, messages, inverse):
    hit, inside = slot_tables(slots)
    live = valid[0:1, :]
    partner = partner_values(vals[0:2, :], sided(parity, messages)) * live
    springs = stiffness_rows(stiffness)
    coupled = scatter((partner[0:1], partner[1:2]), hit, inside)
    result = (springs * neighbour_sum(field[...]) + coupled) * inverse[...]
    return result, jnp.concatenate(gather(result, hit, inside), 0), springs


def step_kernel(parity, stiffness, slots, valid, inverse, field, vals, m1, m2, m3, m4, field_ref, vals_ref):
    result, found, _ = advance(
        parity, stiffness, slots, valid, field, vals, (m1, m2, m3, m4), inverse
    )
    field_ref[...] = result
    vals_ref[...] = padded(found)


def moments_kernel(parity, stiffness, slots, valid, inverse, first, field, vals, m1, m2, m3, m4, field_ref, send_ref):
    third, found, springs = advance(
        parity, stiffness, slots, valid, field, vals, (m1, m2, m3, m4), inverse
    )
    field_ref[...] = third
    w0, w1 = first[...], field[...]
    diagonal = 1.0 / inverse[...]
    products = [
        w0 * w0 * diagonal,
        w0 * w1 * diagonal,
        w1 * w1 * diagonal,
        w1 * third * diagonal,
        third * third * diagonal,
        third * springs * neighbour_sum(third),
    ]
    sums = jnp.concatenate(
        [jnp.sum(p, axis=0, keepdims=True) for p in products] + [jnp.zeros((2, W), f32)], 0
    )
    live = valid[0:1, :]
    found = found * live
    lane, kind, _ = lane_kinds((2, W))
    crossed = jnp.where((lane < SLOTS) & (kind == 4), found * pltpu.roll(found, W - SLOTS, 1), 0.0)
    row8 = lax.broadcasted_iota(jnp.int32, (8, W), 0)
    lane8 = lax.broadcasted_iota(jnp.int32, (8, W), 1)
    sums = sums + jnp.where(row8 == 5, 2.0 * jnp.sum(crossed, axis=0, keepdims=True), 0.0)
    moments = jnp.sum(
        jnp.where(lane8 == 2 * SLOTS + row8, jnp.sum(sums, axis=1, keepdims=True), 0.0),
        axis=0,
        keepdims=True,
    )
    forward = jnp.where(((kind == 0) | (kind == 2)) & (lane < 2 * SLOTS), found, 0.0)
    backward = jnp.where(((kind == 1) | (kind == 3)) & (lane < 2 * SLOTS), found, 0.0)
    sent = forward[0:1] + pltpu.roll(forward, P_SIZE, 1)[1:2] + moments
    answer = pltpu.roll(backward, W - P_SIZE, 1)[0:1] + backward[1:2]
    block = jnp.where(row8 % 2 == 0, sent, answer)
    for t in range(send_ref.shape[0] // 8):
        send_ref[t * 8 : (t + 1) * 8, :] = block


def finish_kernel(columns, gathered, first, second, third, out_ref):
    count = gathered.shape[0] // 2
    sent = gathered[pl.ds(0, count, stride=2), :]
    answer = gathered[pl.ds(1, count, stride=2), :]
    lane = lax.broadcasted_iota(jnp.int32, (count, W), 1)
    within = jnp.where(lane < SLOTS, lane, lane - SLOTS)
    facing = jnp.where(
        within < 2 * P_SIZE,
        pltpu.roll(answer, count - 1, 0),
        pltpu.roll(answer, count - columns, 0),
    )
    edges = jnp.where((within < 4 * P_SIZE) & (lane < 2 * SLOTS), sent * facing, 0.0)
    edges = 2.0 * jnp.sum(edges, axis=0, keepdims=True)
    totals = jnp.sum(sent, axis=0, keepdims=True)
    row8 = lax.broadcasted_iota(jnp.int32, (8, W), 0)
    lane8 = lax.broadcasted_iota(jnp.int32, (8, W), 1)
    picked = jnp.where(lane8 == 2 * SLOTS + row8, totals, 0.0) + jnp.where(row8 == 5, edges, 0.0)
    picked = jnp.sum(picked, axis=1, keepdims=True)
    nu = [picked[k : k + 1, :] for k in range(6)]

    def inner(p, q, shifted):
        total = jnp.zeros((1, 1), f32)
        for i, a in enumerate(p):
            for j, b in enumerate(q):
                moment = nu[i + j] - nu[i + j + 1] if shifted else nu[i + j]
                total = total + a * b * moment
        return total

    def add(p, q, factor):
        length = max(len(p), len(q))
        zero = jnp.zeros((1, 1), f32)
        p = p + [zero] * (length - len(p))
        q = q + [zero] * (length - len(q))
        return [a + factor * b for a, b in zip(p, q)]

    one = jnp.ones((1, 1), f32)
    residual, direction, solution = [one], [one], [jnp.zeros((1, 1), f32)]
    norm = inner(residual, residual, False)
    for iteration in range(3):
        step = norm / inner(direction, direction, True)
        solution = add(solution, direction, step)
        if iteration == 2:
            break
        moved = [-d for d in direction]
        image = add(direction + [jnp.zeros((1, 1), f32)], [jnp.zeros((1, 1), f32)] + moved, one)
        residual = add(residual, image, -step)
        latest = inner(residual, residual, False)
        direction = add(residual, direction, latest / norm)
        norm = latest
    out_ref[...] = solution[0] * first[...] + solution[1] * second[...] + solution[2] * third[...]


SMEM = pl.BlockSpec(memory_space=pltpu.SMEM)
VMEM = pl.BlockSpec(memory_space=pltpu.VMEM)


def shaped(*shapes):
    return [jax.ShapeDtypeStruct(s, f32) for s in shapes]


def local(columns, rows, strips, centers, match_lists, match_counts, spring_stiffness):
    tables = [jnp.asarray(t) for t in fourier_tables()]
    parity_x, parity_y = lax.axis_index("tx") % 2, lax.axis_index("ty") % 2
    parity = jnp.stack([parity_x, parity_y]).astype(jnp.int32)
    sides = jnp.stack([parity_x, 1 - parity_x, 2 + parity_y, 3 - parity_y]).astype(jnp.int32)

    def swaps(count, odd):
        pairs = [(i, i + 1) for i in range(odd, count - 1, 2)]
        return pairs + [(b, a) for a, b in pairs]

    routes = [
        ("tx", swaps(columns, 0)),
        ("tx", swaps(columns, 1)),
        ("ty", swaps(rows, 0)),
        ("ty", swaps(rows, 1)),
    ]

    def exchange(arrays):
        return [lax.ppermute(a, axis, route) for a, (axis, route) in zip(arrays, routes)]

    outgoing = []
    for number in range(4):
        side = sides[number]
        piece = lax.dynamic_slice(
            strips,
            (0, 0, 0, side, (1 - side % 2) * HALF, 0, 0),
            (2, 1, 1, 1, HALF, W, W),
        )
        outgoing.append(piece.reshape(2, HALF, W, W))
    received = exchange(outgoing)
    cross = cross_offsets(centers, tables)
    edge = edge_offsets(sides, strips, received, tables)

    def on_lanes(values):
        return jnp.pad(values.reshape(1, 2 * SLOTS), ((0, 7), (0, W - 2 * SLOTS)))

    slots = on_lanes(match_lists[..., 0])
    live = jnp.arange(P_SIZE, dtype=jnp.int32) < match_counts[..., None]
    valid = on_lanes(live.astype(f32))
    stiffness = spring_stiffness.reshape(2)

    messages = exchange([edge] * 4)
    first, vals, shift, inverse = pl.pallas_call(
        start_kernel,
        in_specs=[SMEM, SMEM] + [VMEM] * 8,
        out_specs=[VMEM] * 4,
        out_shape=shaped((32, W), (8, W), (8, W), (32, W)),
        name="start",
    )(parity, stiffness, slots, valid, cross, edge, *messages)
    messages = exchange([vals] * 4)
    second, vals = pl.pallas_call(
        step_kernel,
        in_specs=[SMEM, SMEM] + [VMEM] * 9,
        out_specs=[VMEM] * 2,
        out_shape=shaped((32, W), (8, W)),
        name="step",
    )(parity, stiffness, slots, valid, inverse, first, vals, *messages)
    messages = exchange([vals] * 4)
    third, sent = pl.pallas_call(
        moments_kernel,
        in_specs=[SMEM, SMEM] + [VMEM] * 10,
        out_specs=[VMEM] * 2,
        out_shape=shaped((32, W), (2 * rows * columns, W)),
        name="moments",
    )(parity, stiffness, slots, valid, inverse, first, second, vals, *messages)
    gathered = lax.all_to_all(sent, ("ty", "tx"), 0, 0, tiled=True)
    solution = pl.pallas_call(
        functools.partial(finish_kernel, columns),
        in_specs=[VMEM] * 4,
        out_specs=VMEM,
        out_shape=jax.ShapeDtypeStruct((32, W), f32),
        name="finish",
    )(gathered, first, second, third)
    vertex_shift = solution.reshape(2, 2, 1, 1, V * V)
    match_shift = shift[0:2, 0 : 2 * SLOTS].reshape(2, 2, 1, 1, 5, P_SIZE)
    return vertex_shift, match_shift


def solution(mesh):
    return jax.shard_map(
        functools.partial(local, mesh.shape["tx"], mesh.shape["ty"]),
        mesh=mesh,
        in_specs=(
            P(None, "ty", "tx", None, None, None, None),
            P(None, "ty", "tx", None, None, None),
            P(None, "ty", "tx", None, None, None),
            P(None, "ty", "tx", None),
            P(None, "ty", "tx"),
        ),
        out_specs=(P(None, None, "ty", "tx", None), P(None, None, "ty", "tx", None, None)),
        check_vma=False,
    )
```

time: 545 us -> 100 us (0.18); the launches traced: 535 us -> 99.7 us
  blocking collectives: 329 us -> 0 us
  matrix products: 131 us -> 0 us
  Pallas kernels: 0 us -> 30.4 us
  between operations: 8.9 us -> 1.06 us
    psum x5 -> x0, blocking collectives: 329 us -> none  [the longest x3 196 us: global_norm(): return lax.psum(jnp.sum(current * scaled), ('ty', 'tx'))]
    dot_general x106 -> x0, matrix products: 131 us -> none  [the longest x9 15.9 us: spectrum(): jnp.einsum('um,...mv->...uv', sin_table, by_cos, precision=precise)]
    pallas_call x0 -> x6, Pallas kernels: none -> 30.4 us  [the longest x1 17.6 us: edge_offsets(): pl.pallas_call(edge_kernel, grid_spec=pltpu.PrefetchScalarGridSpec(num_sc...]
    all_to_all x0 -> x1, starting transfers between devices: none -> 13.9 us  [local(): gathered = lax.all_to_all(sent, ('ty', 'tx'), 0, 0, tiled=True)]
    ppermute x16, starting transfers between devices: 45 us -> 32.5 us  [exchange(): lax.ppermute(a, axis, route)]
    all_to_all x0 -> x1, waiting for transfers between devices: none -> 8.68 us  [local(): gathered = lax.all_to_all(sent, ('ty', 'tx'), 0, 0, tiled=True)]
    ppermute x16, waiting for transfers between devices: 12.1 us -> 4.69 us  [exchange(): lax.ppermute(a, axis, route)]
  transfers between devices with their start and end apart: 16 -> 17, of which waited for: 6 -> 4; matrix products, arithmetic and copies ran while one was open for 16% -> 4% of each run, Pallas kernels for 0% -> 6%
where the time goes in v1:
time: 100 us; the launch traced here: 99.7 us
  starting transfers between devices  46.4 us (46%)
  Pallas kernels  30.4 us (30%)
  waiting for transfers between devices  13.4 us (13%)
  local copies, waits for them, and re-layouts  6.55 us (7%)
  other arithmetic  1.95 us (2%)
  between operations  1.06 us (1%)
    ppermute x16, starting transfers between devices, exchange(): lax.ppermute(a, axis, route)  32.5 us
    pallas_call x1, Pallas kernels, edge_offsets(): pl.pallas_call(edge_kernel, grid_spec=pltpu.PrefetchScalarGridSpec(num_sc...  17.6 us
    all_to_all x1, starting transfers between devices, local(): gathered = lax.all_to_all(sent, ('ty', 'tx'), 0, 0, tiled=True)  13.9 us
    all_to_all x1, waiting for transfers between devices, local(): gathered = lax.all_to_all(sent, ('ty', 'tx'), 0, 0, tiled=True)  8.68 us
    pallas_call x1, Pallas kernels, cross_offsets(): pl.pallas_call(cross_kernel, grid=(2,), in_specs=[pl.BlockSpec((1, 1, 1,...  5.55 us
    ppermute x16, waiting for transfers between devices, exchange(): lax.ppermute(a, axis, route)  4.69 us
    unnamed x38, local copies, waits for them, and re-layouts  3.11 us
  transfers between devices with their start and end apart: 17, of which 4 were waited for; matrix products, arithmetic and copies ran while one was open for 4% of the time, Pallas kernels for 6%

profile of v1, /device:TPU:1, one launch (start us, length us, event | category | flops | bytes accessed | tf_op | source)
XLA Modules:
  0.0 99.7 jit_solution(14632235448256545544)
XLA Ops:
  0.7 1.3 %dynamic-slice_bitcast_fusion = (bf16[2,4,128,128]{3,2,1,0:T(8,128)(2,1)S(1)}, bf16[2,4,128,128]{3,2,1,0:T(8,128)(2,1)S(1)}, bf16[2,4,128,128]{3,2,1,0:T(8,128)(2,1)S(1)}, bf16[2,4,128,128]{3,2,1,0:T(8,128)(2,1)S(1)}) fusion(bf16[2,1,1,4,8,128,128]{6,5,4,3,2,1,0:T(8,128)(2,1)} %own_ref.3, s32[]{:T(128)S(6)} %select_n.62, s32[]{:T(128)S(6)} %select_n.64, ...), kind=kLoop, calls=%fused_computation | loop fusion | bytes 2097184 | tf_op jit(solution)/shard_map/reshape | solution.py:500
  2.0 2.1 %collective-permute-start = (bf16[2,4,128,128]{3,2,1,0:T(8,128)(2,1)S(1)}, bf16[2,4,128,128]{3,2,1,0:T(8,128)(2,1)S(1)}, u32[]{:S(2)}, u32[]{:S(2)}) collective-permute-start(bf16[2,4,128,128]{3,2,1,0:T(8,128)(2,1)S(1)} %get-tuple-element.25), channel_id=1, source_target_pairs={{0,1},{2,3},{4,5},{6,7},{8,9},{10,11},{12,13},{14,15},{1,0},{3,2},... | collective-permute-start | bytes 786440 | tf_op jit(solution)/shard_map/ppermute | solution.py:490
  4.1 0.7 collective-permute-start.1
  4.8 1.0 %collective-permute-start.2 = (bf16[2,4,128,128]{3,2,1,0:T(8,128)(2,1)S(1)}, bf16[2,4,128,128]{3,2,1,0:T(8,128)(2,1)S(1)}, u32[]{:S(2)}, u32[]{:S(2)}) collective-permute-start(bf16[2,4,128,128]{3,2,1,0:T(8,128)(2,1)S(1)} %get-tuple-element.23), channel_id=1, source_target_pairs={{0,16},{32,48},{64,80},{96,112},{16,0},{48,32},{80,64},{112,96},{1... | collective-permute-start | bytes 786440 | tf_op jit(solution)/shard_map/ppermute | solution.py:490
  5.8 3.4 %collective-permute-start.3 = (bf16[2,4,128,128]{3,2,1,0:T(8,128)(2,1)S(1)}, bf16[2,4,128,128]{3,2,1,0:T(8,128)(2,1)S(1)}, u32[]{:S(2)}, u32[]{:S(2)}) collective-permute-start(bf16[2,4,128,128]{3,2,1,0:T(8,128)(2,1)S(1)} %get-tuple-element.22), channel_id=1, source_target_pairs={{16,32},{48,64},{80,96},{32,16},{64,48},{96,80},{17,33},{49,65},{8... | collective-permute-start | bytes 786440 | tf_op jit(solution)/shard_map/ppermute | solution.py:490
  9.3 0.1 iota_compare_fusion
  9.4 0.7 pad_add_fusion.1.sides
  10.0 0.1 convert_element_type.15
  10.1 0.6 pad_convert_fusion.valid
  10.8 0.0 collective-permute-done.r0
  10.8 0.0 collective-permute-done.1.r1
  10.8 0.0 copy-start.2
  10.8 0.0 collective-permute-done.2.r2
  10.8 2.7 %collective-permute-done.3.r3 = bf16[2,4,128,128]{3,2,1,0:T(8,128)(2,1)S(1)} collective-permute-done((bf16[2,4,128,128]{3,2,1,0:T(8,128)(2,1)S(1)}, bf16[2,4,128,128]{3,2,1,0:T(8,128)(2,1)S(1)}, u32[]{:S(2)}, u32[]{:S(2)}) %collective-permute-start.3) | collective-permute-done | bytes 262176 | tf_op jit(solution)/shard_map/ppermute | solution.py:490
  13.5 0.0 copy-done.3
  13.5 0.0 copy-start.4
  13.5 0.7 copy-done.4
  14.2 17.6 %edge_corr.1.edge = f32[8,128]{1,0:T(8,128)} custom-call(s32[4]{0:T(128)} %pad_add_fusion.1.sides, bf16[2,1,1,4,8,128,128]{6,5,4,3,2,1,0:T(8,128)(2,1)} %own_ref.3, bf16[2,4,128,128]{3,2,1,0:T(8,128)(2,1)} %copy-done.1, bf16[2,4,128,128]{3,2,1,0:T(8,128)(2,1)} %copy-done.2, bf16[2,4,128,128]{3,2,1,0:T(8,128)(2,1)} %copy-done.3, ...), custom_call_target="tpu_custom_call" | custom-call | tf_op jit(solution)/shard_map/edge_corr/pallas_call | solution.py:227
  31.8 3.6 %collective-permute-start.4 = (f32[8,128]{1,0:T(8,128)}, f32[8,128]{1,0:T(8,128)S(1)}, u32[]{:S(2)}, u32[]{:S(2)}) collective-permute-start(f32[8,128]{1,0:T(8,128)} %edge_corr.1.edge), channel_id=1, source_target_pairs={{0,1},{2,3},{4,5},{6,7},{8,9},{10,11},{12,13},{14,15},{1,0},{3,2},... | collective-permute-start | bytes 12296 | tf_op jit(solution)/shard_map/ppermute | solution.py:490
  35.5 0.6 collective-permute-start.5
  36.1 0.1 collective-permute-start.6
  36.2 3.9 %collective-permute-start.7 = (f32[8,128]{1,0:T(8,128)}, f32[8,128]{1,0:T(8,128)S(1)}, u32[]{:S(2)}, u32[]{:S(2)}) collective-permute-start(f32[8,128]{1,0:T(8,128)} %edge_corr.1.edge), channel_id=1, source_target_pairs={{16,32},{48,64},{80,96},{32,16},{64,48},{96,80},{17,33},{49,65},{8... | collective-permute-start | bytes 12296 | tf_op jit(solution)/shard_map/ppermute | solution.py:490
  40.1 0.6 pad_add_fusion.parity
  40.7 0.1 reshape_squeeze.3
  40.8 0.6 pad.10.slots
  41.4 5.5 %cross_corr.1.cross = f32[8,128]{1,0:T(8,128)} custom-call(bf16[2,1,1,8,128,128]{5,4,3,2,1,0:T(8,128)(2,1)} %par_ref.1, bf16[2,1,1,8,128,128]{5,4,3,2,1,0:T(8,128)(2,1)} %par_ref.1, bf16[256,256]{1,0:T(8,128)(2,1)} %constant.71.clone.t1, bf16[288,256]{1,0:T(8,128)(2,1)} %constant.72.clone.t2, bf16[512,256]{1,0:T(8,128)(2,1)} %constant.73.clone.t3, ...), custom_call_target="tpu_custom_call" | custom-call | tf_op jit(solution)/shard_map/cross_corr/pallas_call | solution.py:211
  47.0 0.0 collective-permute-done.4.m1
  47.0 0.0 collective-permute-done.5.m2
  47.0 0.0 collective-permute-done.6.m3
  47.0 0.0 collective-permute-done.7.m4
  47.0 0.0 copy-start.8
  47.0 0.5 copy-done.5
  47.6 0.0 copy-done.7
  47.6 0.0 copy-done.8
  47.6 1.8 %start.1 = (f32[32,128]{1,0:T(8,128)}, f32[8,128]{1,0:T(8,128)}, f32[8,128]{1,0:T(8,128)}, f32[32,128]{1,0:T(8,128)}) custom-call(s32[2]{0:T(128)} %pad_add_fusion.parity, f32[2]{0:T(128)} %bitcast.23, s32[8,128]{1,0:T(8,128)} %pad.10.slots, f32[8,128]{1,0:T(8,128)} %pad_convert_fusion.valid, f32[8,128]{1,0:T(8,128)} %cross_corr.1.cross, ...), custom_call_target="tpu_custom_call" | custom-call | tf_op jit(solution)/shard_map/start/pallas_call | solution.py:514
  49.4 0.0 collective-permute-start.10
  49.4 3.9 %collective-permute-start.11 = (f32[8,128]{1,0:T(8,128)}, f32[8,128]{1,0:T(8,128)S(1)}, u32[]{:S(2)}, u32[]{:S(2)}) collective-permute-start(f32[8,128]{1,0:T(8,128)} %get-tuple-element.12.vals), channel_id=1, source_target_pairs={{16,32},{48,64},{80,96},{32,16},{64,48},{96,80},{17,33},{49,65},{8... | collective-permute-start | bytes 12296 | tf_op jit(solution)/shard_map/ppermute | solution.py:490
  53.3 4.5 %collective-permute-start.8 = (f32[8,128]{1,0:T(8,128)}, f32[8,128]{1,0:T(8,128)S(1)}, u32[]{:S(2)}, u32[]{:S(2)}) collective-permute-start(f32[8,128]{1,0:T(8,128)} %get-tuple-element.12.vals), channel_id=1, source_target_pairs={{0,1},{2,3},{4,5},{6,7},{8,9},{10,11},{12,13},{14,15},{1,0},{3,2},... | collective-permute-start | bytes 12296 | tf_op jit(solution)/shard_map/ppermute | solution.py:490
  57.9 0.6 collective-permute-start.9
  58.5 0.0 collective-permute-done.10.m3
  58.5 0.0 collective-permute-done.11.m4
  58.6 0.5 collective-permute-done.8.m1
  59.1 0.0 collective-permute-done.9.m2
  59.1 0.0 copy-done.13
  59.1 0.0 copy-done.14
  59.1 0.5 copy-done.15
  59.7 1.8 %step.1 = (f32[32,128]{1,0:T(8,128)}, f32[8,128]{1,0:T(8,128)}) custom-call(s32[2]{0:T(128)} %pad_add_fusion.parity, f32[2]{0:T(128)} %bitcast.24, s32[8,128]{1,0:T(8,128)} %pad.10.slots, f32[8,128]{1,0:T(8,128)} %pad_convert_fusion.valid, f32[32,128]{1,0:T(8,128)} %get-tuple-element.10.inverse, f32[32,128]{1,0:T(8,128)} %get-tuple-element.11.field.first, ...), custom_call_target="tpu_custom_call" | custom-call | tf_op jit(solution)/shard_map/step/pallas_call | solution.py:522
  61.4 3.5 %collective-permute-start.12 = (f32[8,128]{1,0:T(8,128)}, f32[8,128]{1,0:T(8,128)S(1)}, u32[]{:S(2)}, u32[]{:S(2)}) collective-permute-start(f32[8,128]{1,0:T(8,128)} %get-tuple-element.14.vals), channel_id=1, source_target_pairs={{0,1},{2,3},{4,5},{6,7},{8,9},{10,11},{12,13},{14,15},{1,0},{3,2},... | collective-permute-start | bytes 12296 | tf_op jit(solution)/shard_map/ppermute | solution.py:490
  64.9 0.6 collective-permute-start.13
  65.6 0.1 collective-permute-start.14
  65.6 3.6 %collective-permute-start.15 = (f32[8,128]{1,0:T(8,128)}, f32[8,128]{1,0:T(8,128)S(1)}, u32[]{:S(2)}, u32[]{:S(2)}) collective-permute-start(f32[8,128]{1,0:T(8,128)} %get-tuple-element.14.vals), channel_id=1, source_target_pairs={{16,32},{48,64},{80,96},{32,16},{64,48},{96,80},{17,33},{49,65},{8... | collective-permute-start | bytes 12296 | tf_op jit(solution)/shard_map/ppermute | solution.py:490
  69.3 0.0 collective-permute-done.12.m1
  69.3 0.0 collective-permute-done.13.m2
  69.3 0.0 collective-permute-done.14.m3
  69.3 0.0 copy-start.11
  69.3 1.4 %collective-permute-done.15.m4 = f32[8,128]{1,0:T(8,128)S(1)} collective-permute-done((f32[8,128]{1,0:T(8,128)}, f32[8,128]{1,0:T(8,128)S(1)}, u32[]{:S(2)}, u32[]{:S(2)}) %collective-permute-start.15) | collective-permute-done | bytes 4128 | tf_op jit(solution)/shard_map/ppermute | solution.py:490
  70.8 0.6 copy-done.12
  71.4 2.0 %moments.1 = (f32[32,128]{1,0:T(8,128)}, f32[256,128]{1,0:T(8,128)}) custom-call(s32[2]{0:T(128)} %pad_add_fusion.parity, f32[2]{0:T(128)} %bitcast.25, s32[8,128]{1,0:T(8,128)} %pad.10.slots, f32[8,128]{1,0:T(8,128)} %pad_convert_fusion.valid, f32[32,128]{1,0:T(8,128)} %get-tuple-element.10.inverse, f32[32,128]{1,0:T(8,128)} %get-tuple-element.11.field.first, ...), custom_call_target="tpu_custom_call" | custom-call | tf_op jit(solution)/shard_map/moments/pallas_call | solution.py:530
  73.4 13.9 %all-to-all-start = ((f32[128,2,128]{2,1,0:T(2,128)}), f32[128,2,128]{2,1,0:T(2,128)S(1)}, u32[]{:S(2)}, u32[]{:S(2)}) async-start(f32[128,2,128]{2,1,0:T(2,128)} %bitcast.21), calls=%async_computation | async-start | bytes 262144 | tf_op jit(solution)/shard_map/all_to_all | solution.py:537
  87.3 0.7 slice.7
  88.0 0.7 reshape.68
  88.7 8.7 %all-to-all-done = f32[128,2,128]{2,1,0:T(2,128)S(1)} async-done(((f32[128,2,128]{2,1,0:T(2,128)}), f32[128,2,128]{2,1,0:T(2,128)S(1)}, u32[]{:S(2)}, u32[]{:S(2)}) %all-to-all-start) | async-done | bytes 131104 | tf_op jit(solution)/shard_map/all_to_all | solution.py:537
  97.3 0.6 copy-done
  98.0 1.7 %finish.1 = f32[32,128]{1,0:T(8,128)} custom-call(f32[256,128]{1,0:T(8,128)} %bitcast.20, f32[32,128]{1,0:T(8,128)} %get-tuple-element.11.field.first, f32[32,128]{1,0:T(8,128)} %get-tuple-element.13.field.second, f32[32,128]{1,0:T(8,128)} %get-tuple-element.16.third), custom_call_target="tpu_custom_call" | custom-call | tf_op jit(solution)/shard_map/finish/pallas_call | solution.py:538
  (25 shorter events, 0.1 us)
Async XLA Ops:
  0.6 8.7 %copy-start.18 = (s32[2,1,1,5]{3,2,1,0:T(1,128)S(1)}, s32[2,1,1,5]{3,2,1,0:T(1,128)}, u32[]{:S(2)}) copy-start(s32[2,1,1,5]{3,2,1,0:T(1,128)} %param.14) | copy-start | bytes 124
  0.6 10.1 %copy-start.17 = (s32[2,1,1,5,8,2]{4,5,3,2,1,0:T(2,128)S(1)}, s32[2,1,1,5,8,2]{4,5,3,2,1,0:T(2,128)}, u32[]{:S(2)}) copy-start(s32[2,1,1,5,8,2]{4,5,3,2,1,0:T(2,128)} %param.13) | copy-start | bytes 1924
  2.0 8.7 %collective-permute-start = (bf16[2,4,128,128]{3,2,1,0:T(8,128)(2,1)S(1)}, bf16[2,4,128,128]{3,2,1,0:T(8,128)(2,1)S(1)}, u32[]{:S(2)}, u32[]{:S(2)}) collective-permute-start(bf16[2,4,128,128]{3,2,1,0:T(8,128)(2,1)S(1)} %get-tuple-element.25), channel_id=1, source_target_pairs={{0,1},{2,3},{4,5},{6,7},{8,9},{10,11},{12,13},{14,15},{1,0},{3,2},... | collective-permute-start | bytes 786440 | tf_op jit(solution)/shard_map/ppermute | solution.py:490
  4.1 6.6 %collective-permute-start.1 = (bf16[2,4,128,128]{3,2,1,0:T(8,128)(2,1)S(1)}, bf16[2,4,128,128]{3,2,1,0:T(8,128)(2,1)S(1)}, u32[]{:S(2)}, u32[]{:S(2)}) collective-permute-start(bf16[2,4,128,128]{3,2,1,0:T(8,128)(2,1)S(1)} %get-tuple-element.24), channel_id=1, source_target_pairs={{1,2},{3,4},{5,6},{7,8},{9,10},{11,12},{13,14},{2,1},{4,3},{6,5},{... | collective-permute-start | bytes 786440 | tf_op jit(solution)/shard_map/ppermute | solution.py:490
  4.8 6.0 %collective-permute-start.2 = (bf16[2,4,128,128]{3,2,1,0:T(8,128)(2,1)S(1)}, bf16[2,4,128,128]{3,2,1,0:T(8,128)(2,1)S(1)}, u32[]{:S(2)}, u32[]{:S(2)}) collective-permute-start(bf16[2,4,128,128]{3,2,1,0:T(8,128)(2,1)S(1)} %get-tuple-element.23), channel_id=1, source_target_pairs={{0,16},{32,48},{64,80},{96,112},{16,0},{48,32},{80,64},{112,96},{1... | collective-permute-start | bytes 786440 | tf_op jit(solution)/shard_map/ppermute | solution.py:490
  5.8 7.7 %collective-permute-start.3 = (bf16[2,4,128,128]{3,2,1,0:T(8,128)(2,1)S(1)}, bf16[2,4,128,128]{3,2,1,0:T(8,128)(2,1)S(1)}, u32[]{:S(2)}, u32[]{:S(2)}) collective-permute-start(bf16[2,4,128,128]{3,2,1,0:T(8,128)(2,1)S(1)} %get-tuple-element.22), channel_id=1, source_target_pairs={{16,32},{48,64},{80,96},{32,16},{64,48},{96,80},{17,33},{49,65},{8... | collective-permute-start | bytes 786440 | tf_op jit(solution)/shard_map/ppermute | solution.py:490
  10.8 2.8 %copy-start.1 = (bf16[2,4,128,128]{3,2,1,0:T(8,128)(2,1)}, bf16[2,4,128,128]{3,2,1,0:T(8,128)(2,1)S(1)}, u32[]{:S(2)}) copy-start(bf16[2,4,128,128]{3,2,1,0:T(8,128)(2,1)S(1)} %collective-permute-done.r0) | copy-start | bytes 786436
  10.8 2.7 %copy-start.2 = (bf16[2,4,128,128]{3,2,1,0:T(8,128)(2,1)}, bf16[2,4,128,128]{3,2,1,0:T(8,128)(2,1)S(1)}, u32[]{:S(2)}) copy-start(bf16[2,4,128,128]{3,2,1,0:T(8,128)(2,1)S(1)} %collective-permute-done.1.r1) | copy-start | bytes 786436
  10.8 2.7 %copy-start.3 = (bf16[2,4,128,128]{3,2,1,0:T(8,128)(2,1)}, bf16[2,4,128,128]{3,2,1,0:T(8,128)(2,1)S(1)}, u32[]{:S(2)}) copy-start(bf16[2,4,128,128]{3,2,1,0:T(8,128)(2,1)S(1)} %collective-permute-done.2.r2) | copy-start | bytes 786436
  13.5 0.7 copy-start.4
  31.8 15.2 %collective-permute-start.4 = (f32[8,128]{1,0:T(8,128)}, f32[8,128]{1,0:T(8,128)S(1)}, u32[]{:S(2)}, u32[]{:S(2)}) collective-permute-start(f32[8,128]{1,0:T(8,128)} %edge_corr.1.edge), channel_id=1, source_target_pairs={{0,1},{2,3},{4,5},{6,7},{8,9},{10,11},{12,13},{14,15},{1,0},{3,2},... | collective-permute-start | bytes 12296 | tf_op jit(solution)/shard_map/ppermute | solution.py:490
  35.5 11.5 %collective-permute-start.5 = (f32[8,128]{1,0:T(8,128)}, f32[8,128]{1,0:T(8,128)S(1)}, u32[]{:S(2)}, u32[]{:S(2)}) collective-permute-start(f32[8,128]{1,0:T(8,128)} %edge_corr.1.edge), channel_id=1, source_target_pairs={{1,2},{3,4},{5,6},{7,8},{9,10},{11,12},{13,14},{2,1},{4,3},{6,5},{... | collective-permute-start | bytes 12296 | tf_op jit(solution)/shard_map/ppermute | solution.py:490
  36.1 10.9 %collective-permute-start.6 = (f32[8,128]{1,0:T(8,128)}, f32[8,128]{1,0:T(8,128)S(1)}, u32[]{:S(2)}, u32[]{:S(2)}) collective-permute-start(f32[8,128]{1,0:T(8,128)} %edge_corr.1.edge), channel_id=1, source_target_pairs={{0,16},{32,48},{64,80},{96,112},{16,0},{48,32},{80,64},{112,96},{1... | collective-permute-start | bytes 12296 | tf_op jit(solution)/shard_map/ppermute | solution.py:490
  36.2 10.8 %collective-permute-start.7 = (f32[8,128]{1,0:T(8,128)}, f32[8,128]{1,0:T(8,128)S(1)}, u32[]{:S(2)}, u32[]{:S(2)}) collective-permute-start(f32[8,128]{1,0:T(8,128)} %edge_corr.1.edge), channel_id=1, source_target_pairs={{16,32},{48,64},{80,96},{32,16},{64,48},{96,80},{17,33},{49,65},{8... | collective-permute-start | bytes 12296 | tf_op jit(solution)/shard_map/ppermute | solution.py:490
  47.0 0.6 copy-start.5
  47.0 0.6 copy-start.6
  47.0 0.6 copy-start.7
  47.0 0.6 copy-start.8
  49.4 9.2 %collective-permute-start.10 = (f32[8,128]{1,0:T(8,128)}, f32[8,128]{1,0:T(8,128)S(1)}, u32[]{:S(2)}, u32[]{:S(2)}) collective-permute-start(f32[8,128]{1,0:T(8,128)} %get-tuple-element.12.vals), channel_id=1, source_target_pairs={{0,16},{32,48},{64,80},{96,112},{16,0},{48,32},{80,64},{112,96},{1... | collective-permute-start | bytes 12296 | tf_op jit(solution)/shard_map/ppermute | solution.py:490
  49.4 9.2 %collective-permute-start.11 = (f32[8,128]{1,0:T(8,128)}, f32[8,128]{1,0:T(8,128)S(1)}, u32[]{:S(2)}, u32[]{:S(2)}) collective-permute-start(f32[8,128]{1,0:T(8,128)} %get-tuple-element.12.vals), channel_id=1, source_target_pairs={{16,32},{48,64},{80,96},{32,16},{64,48},{96,80},{17,33},{49,65},{8... | collective-permute-start | bytes 12296 | tf_op jit(solution)/shard_map/ppermute | solution.py:490
  53.3 5.8 %collective-permute-start.8 = (f32[8,128]{1,0:T(8,128)}, f32[8,128]{1,0:T(8,128)S(1)}, u32[]{:S(2)}, u32[]{:S(2)}) collective-permute-start(f32[8,128]{1,0:T(8,128)} %get-tuple-element.12.vals), channel_id=1, source_target_pairs={{0,1},{2,3},{4,5},{6,7},{8,9},{10,11},{12,13},{14,15},{1,0},{3,2},... | collective-permute-start | bytes 12296 | tf_op jit(solution)/shard_map/ppermute | solution.py:490
  57.9 1.2 %collective-permute-start.9 = (f32[8,128]{1,0:T(8,128)}, f32[8,128]{1,0:T(8,128)S(1)}, u32[]{:S(2)}, u32[]{:S(2)}) collective-permute-start(f32[8,128]{1,0:T(8,128)} %get-tuple-element.12.vals), channel_id=1, source_target_pairs={{1,2},{3,4},{5,6},{7,8},{9,10},{11,12},{13,14},{2,1},{4,3},{6,5},{... | collective-permute-start | bytes 12296 | tf_op jit(solution)/shard_map/ppermute | solution.py:490
  58.5 0.6 copy-start.13
  58.6 0.6 copy-start.14
  59.1 0.6 copy-start.15
  59.1 0.6 copy-start.16
  61.4 7.9 %collective-permute-start.12 = (f32[8,128]{1,0:T(8,128)}, f32[8,128]{1,0:T(8,128)S(1)}, u32[]{:S(2)}, u32[]{:S(2)}) collective-permute-start(f32[8,128]{1,0:T(8,128)} %get-tuple-element.14.vals), channel_id=1, source_target_pairs={{0,1},{2,3},{4,5},{6,7},{8,9},{10,11},{12,13},{14,15},{1,0},{3,2},... | collective-permute-start | bytes 12296 | tf_op jit(solution)/shard_map/ppermute | solution.py:490
  64.9 4.4 %collective-permute-start.13 = (f32[8,128]{1,0:T(8,128)}, f32[8,128]{1,0:T(8,128)S(1)}, u32[]{:S(2)}, u32[]{:S(2)}) collective-permute-start(f32[8,128]{1,0:T(8,128)} %get-tuple-element.14.vals), channel_id=1, source_target_pairs={{1,2},{3,4},{5,6},{7,8},{9,10},{11,12},{13,14},{2,1},{4,3},{6,5},{... | collective-permute-start | bytes 12296 | tf_op jit(solution)/shard_map/ppermute | solution.py:490
  65.6 3.8 %collective-permute-start.14 = (f32[8,128]{1,0:T(8,128)}, f32[8,128]{1,0:T(8,128)S(1)}, u32[]{:S(2)}, u32[]{:S(2)}) collective-permute-start(f32[8,128]{1,0:T(8,128)} %get-tuple-element.14.vals), channel_id=1, source_target_pairs={{0,16},{32,48},{64,80},{96,112},{16,0},{48,32},{80,64},{112,96},{1... | collective-permute-start | bytes 12296 | tf_op jit(solution)/shard_map/ppermute | solution.py:490
  65.6 5.1 %collective-permute-start.15 = (f32[8,128]{1,0:T(8,128)}, f32[8,128]{1,0:T(8,128)S(1)}, u32[]{:S(2)}, u32[]{:S(2)}) collective-permute-start(f32[8,128]{1,0:T(8,128)} %get-tuple-element.14.vals), channel_id=1, source_target_pairs={{16,32},{48,64},{80,96},{32,16},{64,48},{96,80},{17,33},{49,65},{8... | collective-permute-start | bytes 12296 | tf_op jit(solution)/shard_map/ppermute | solution.py:490
  69.3 1.5 %copy-start.9 = (f32[8,128]{1,0:T(8,128)}, f32[8,128]{1,0:T(8,128)S(1)}, u32[]{:S(2)}) copy-start(f32[8,128]{1,0:T(8,128)S(1)} %collective-permute-done.12.m1) | copy-start | bytes 12292
  69.3 1.5 %copy-start.10 = (f32[8,128]{1,0:T(8,128)}, f32[8,128]{1,0:T(8,128)S(1)}, u32[]{:S(2)}) copy-start(f32[8,128]{1,0:T(8,128)S(1)} %collective-permute-done.13.m2) | copy-start | bytes 12292
  69.3 1.5 %copy-start.11 = (f32[8,128]{1,0:T(8,128)}, f32[8,128]{1,0:T(8,128)S(1)}, u32[]{:S(2)}) copy-start(f32[8,128]{1,0:T(8,128)S(1)} %collective-permute-done.14.m3) | copy-start | bytes 12292
  70.8 0.6 copy-start.12
  73.4 24.0 %all-to-all-start = ((f32[128,2,128]{2,1,0:T(2,128)}), f32[128,2,128]{2,1,0:T(2,128)S(1)}, u32[]{:S(2)}, u32[]{:S(2)}) async-start(f32[128,2,128]{2,1,0:T(2,128)} %bitcast.21), calls=%async_computation | async-start | bytes 262144 | tf_op jit(solution)/shard_map/all_to_all | solution.py:537
  97.3 0.6 copy-start

commit v2 on v1

--- a/solution.py
+++ b/solution.py
@@ -19,6 +19,10 @@
 epsilon = 1e-06
 f32 = jnp.float32
 bf16 = jnp.bfloat16
+SMEM = pl.BlockSpec(memory_space=pltpu.SMEM)
+VMEM = pl.BlockSpec(memory_space=pltpu.VMEM)
+CORR_VMEM = 16 * 2**20
+SMALL = pltpu.CompilerParams(vmem_limit_bytes=2 * 2**20)
 
 
 def split_table(table):
@@ -68,65 +72,63 @@
     return jnp.dot(left, right, preferred_element_type=f32)
 
 
-def correlate_two(own, partner, tables, high_ref, low_ref):
+def correlate(own, partner, tables, high_ref, low_ref, tot_ref, row_ref):
     along_cols, along_rows, back_cols, back_rows, lag_rows = tables
-    spectra = []
+    groups = P_SIZE // 2
     for side, patches in enumerate((own, partner)):
-        for t, patch in enumerate(patches):
-            high, low = high_low(dot(jnp.concatenate([patch, patch], 1), along_cols[...]))
-            lanes = pl.ds(t * W, W)
-            high_ref[side, 0:W, lanes] = high[:, :W]
-            high_ref[side, W : 2 * W, lanes] = high[:, W:]
-            low_ref[side, 0:W, lanes] = low[:, :W]
-            low_ref[side, W : 2 * W, lanes] = low[:, W:]
-        both = dot(along_rows[...], high_ref[side])
-        spectra.append(
-            both[: 2 * U] + both[2 * U :] + dot(along_rows[0 : 2 * U], low_ref[side])
+        high, low = high_low(dot(jnp.concatenate([patches, patches], 1), along_cols[...]))
+        for j in range(P_SIZE):
+            g, lanes = j // 2, pl.ds(j % 2 * W, W)
+            for ref, part in ((high_ref, high), (low_ref, low)):
+                ref[g, side, 0:W, lanes] = part[j * W : (j + 1) * W, :W]
+                ref[g, side, W : 2 * W, lanes] = part[j * W : (j + 1) * W, W:]
+    highs, lows = [], []
+    for g in range(groups):
+        spectra = []
+        for side in range(2):
+            both = dot(along_rows[...], high_ref[g, side])
+            spectra.append(
+                both[: 2 * U] + both[2 * U :] + dot(along_rows[0 : 2 * U], low_ref[g, side])
+            )
+        own_re, own_im = spectra[0][:U], spectra[0][U:]
+        par_re, par_im = spectra[1][:U], spectra[1][U:]
+        cross_re = own_re * par_re + own_im * par_im
+        cross_im = own_im * par_re - own_re * par_im
+        cross = jnp.concatenate(
+            [
+                jnp.concatenate([cross_re[:, :W], cross_im[:, :W]], 1),
+                jnp.concatenate([cross_re[:, W:], cross_im[:, W:]], 1),
+            ],
+            0,
         )
-    own_re, own_im = spectra[0][:U], spectra[0][U:]
-    par_re, par_im = spectra[1][:U], spectra[1][U:]
-    cross_re = own_re * par_re + own_im * par_im
-    cross_im = own_im * par_re - own_re * par_im
-    cross = jnp.concatenate(
-        [
-            jnp.concatenate([cross_re[:, :W], cross_im[:, :W]], 1),
-            jnp.concatenate([cross_re[:, W:], cross_im[:, W:]], 1),
-        ],
-        0,
-    )
-    high, low = high_low(cross)
-    both = dot(jnp.concatenate([high, low], 0), back_cols[0 : 2 * W])
-    partly = both[: 2 * U] + both[2 * U :] + dot(high, back_cols[2 * W : 4 * W])
+        high, low = high_low(cross)
+        highs.append(high)
+        lows.append(low)
+    count = 2 * U * groups
+    both = dot(jnp.concatenate(highs + lows, 0), back_cols[0 : 2 * W])
+    partly = both[:count] + both[count:]
+    partly = partly + dot(jnp.concatenate(highs, 0), back_cols[2 * W : 4 * W])
     first = lax.broadcasted_iota(jnp.int32, (8, W), 0) == 0
-    stacked = []
-    for t in range(2):
-        real, imag = partly[t * U : (t + 1) * U, :W], partly[t * U : (t + 1) * U, W:]
-        top = jnp.where(first, real[W // 2 : W // 2 + 8], imag[0:8])
-        stacked.append(jnp.concatenate([real[: W // 2], top, imag[8 : W // 2]], 0))
-    high, low = high_low(jnp.concatenate(stacked, 1))
-    surface = dot(back_rows[:, 0 : 2 * W], jnp.concatenate([high, low], 0)) + dot(
-        back_rows[:, 2 * W : 3 * W], high
-    )
-    squared = surface * surface
-    weight = squared * squared
     lagged = lag_rows[...]
-    totals = jnp.sum(weight, axis=0, keepdims=True)
-    rowwise = jnp.sum(weight * jnp.concatenate([lagged, lagged], 1), axis=0, keepdims=True)
-    return totals, rowwise
-
-
-def correlate_four(load_own, load_partner, tables, high_ref, low_ref, tot_ref, row_ref, base):
-    for g in range(2):
-        totals, rowwise = correlate_two(
-            [load_own(2 * g), load_own(2 * g + 1)],
-            [load_partner(2 * g), load_partner(2 * g + 1)],
-            tables,
-            high_ref.at[g],
-            low_ref.at[g],
+    lagged = jnp.concatenate([lagged, lagged], 1)
+    for g in range(groups):
+        stacked = []
+        for t in range(2):
+            piece = partly[(2 * g + t) * U : (2 * g + t + 1) * U]
+            real, imag = piece[:, :W], piece[:, W:]
+            top = jnp.where(first, real[W // 2 : W // 2 + 8], imag[0:8])
+            stacked.append(jnp.concatenate([real[: W // 2], top, imag[8 : W // 2]], 0))
+        high, low = high_low(jnp.concatenate(stacked, 1))
+        surface = dot(back_rows[:, 0 : 2 * W], jnp.concatenate([high, low], 0)) + dot(
+            back_rows[:, 2 * W : 3 * W], high
         )
+        squared = surface * surface
+        weight = squared * squared
+        totals = jnp.sum(weight, axis=0, keepdims=True)
+        rowwise = jnp.sum(weight * lagged, axis=0, keepdims=True)
         for t in range(2):
-            tot_ref[pl.ds(base + 2 * g + t, 1), :] = totals[:, t * W : (t + 1) * W]
-            row_ref[pl.ds(base + 2 * g + t, 1), :] = rowwise[:, t * W : (t + 1) * W]
+            tot_ref[pl.ds(2 * g + t, 1), :] = totals[:, t * W : (t + 1) * W]
+            row_ref[pl.ds(2 * g + t, 1), :] = rowwise[:, t * W : (t + 1) * W]
 
 
 def offsets_on_lanes(tot_ref, row_ref, lag_cols, targets):
@@ -144,105 +146,58 @@
     return jnp.concatenate(rows + [jnp.zeros((6, W), f32)], 0)
 
 
-def cross_kernel(own_ref, par_ref, t1, t2, t3, t4, t5, lag_cols, out_ref, high_ref, low_ref, tot_ref, row_ref):
-    step = pl.program_id(0)
-    correlate_four(
-        lambda j: own_ref[0, 0, 0, j],
-        lambda j: par_ref[0, 0, 0, j],
+def cross_kernel(pixels, t1, t2, t3, t4, t5, lag_cols, out_ref, high_ref, low_ref, tot_ref, row_ref):
+    correlate(
+        pixels[0, 0, 0].reshape(P_SIZE * W, W),
+        pixels[1, 0, 0].reshape(P_SIZE * W, W),
         (t1, t2, t3, t4, t5),
         high_ref,
         low_ref,
         tot_ref,
         row_ref,
-        step * HALF,
-    )
-
-    @pl.when(step == 1)
-    def _():
-        targets = 4 * P_SIZE + lax.broadcasted_iota(jnp.int32, (P_SIZE, W), 0)
-        offset = offsets_on_lanes(tot_ref, row_ref, lag_cols, targets)
-        out_ref[...] = offset - pltpu.roll(offset, SLOTS, 1)
-
-
-def edge_kernel(sides, own_ref, r0, r1, r2, r3, t1, t2, t3, t4, t5, lag_cols, out_ref, par_ref, high_ref, low_ref, tot_ref, row_ref):
-    which, section = pl.program_id(0), pl.program_id(1)
-    for number, ref in enumerate((r0, r1, r2, r3)):
-
-        @pl.when(which == number)
-        def _():
-            par_ref[...] = ref[section]
-
-    correlate_four(
-        lambda j: own_ref[0, 0, 0, 0, j],
-        lambda j: par_ref[j],
+    )
+    targets = 4 * P_SIZE + lax.broadcasted_iota(jnp.int32, (P_SIZE, W), 0)
+    offset = offsets_on_lanes(tot_ref, row_ref, lag_cols, targets)
+    out_ref[...] = offset - pltpu.roll(offset, SLOTS, 1)
+
+
+def side_of(number):
+    place = lax.axis_index("tx" if number < 2 else "ty")
+    return 2 * (number // 2) + lax.rem(place + number, 2)
+
+
+def edge_kernel(number, strips, received, t1, t2, t3, t4, t5, lag_cols, out_ref, high_ref, low_ref, tot_ref, row_ref):
+    side = side_of(number)
+    start = lax.rem(side, 2) * HALF
+    correlate(
+        strips[:, 0, 0, side, pl.ds(start, HALF)].reshape(P_SIZE * W, W),
+        received[...].reshape(P_SIZE * W, W),
         (t1, t2, t3, t4, t5),
         high_ref,
         low_ref,
         tot_ref,
         row_ref,
-        which * P_SIZE + section * HALF,
-    )
-
-    @pl.when((which == 3) & (section == 1))
-    def _():
-        pair = lax.broadcasted_iota(jnp.int32, (4 * P_SIZE, W), 0)
-        start = jnp.zeros_like(pair)
-        for number in range(4):
-            side = sides[number]
-            start = jnp.where(pair // P_SIZE == number, side * P_SIZE + (side % 2) * HALF, start)
-        targets = start + (pair % P_SIZE) // HALF * SLOTS + pair % HALF
-        out_ref[...] = offsets_on_lanes(tot_ref, row_ref, lag_cols, targets)
-
-
-def corr_scratch(pairs):
-    return [
-        pltpu.VMEM((2, 2, 2 * W, 2 * W), bf16),
-        pltpu.VMEM((2, 2, 2 * W, 2 * W), bf16),
-        pltpu.VMEM((pairs, W), f32),
-        pltpu.VMEM((pairs, W), f32),
-    ]
-
-
-def whole(array):
-    return pl.BlockSpec(array.shape, lambda *_: (0,) * array.ndim)
-
-
-def cross_offsets(centers, tables):
+    )
+    pair = lax.broadcasted_iota(jnp.int32, (P_SIZE, W), 0)
+    targets = side * P_SIZE + start + pair // HALF * SLOTS + pair % HALF
+    out_ref[...] = offsets_on_lanes(tot_ref, row_ref, lag_cols, targets)
+
+
+def corr_call(kernel, name, *args):
     return pl.pallas_call(
-        cross_kernel,
-        grid=(2,),
-        in_specs=[
-            pl.BlockSpec((1, 1, 1, HALF, W, W), lambda i: (0, 0, 0, i, 0, 0)),
-            pl.BlockSpec((1, 1, 1, HALF, W, W), lambda i: (1, 0, 0, i, 0, 0)),
-        ]
-        + [whole(t) for t in tables],
-        out_specs=pl.BlockSpec((8, W), lambda i: (0, 0)),
+        kernel,
+        in_specs=[VMEM] * len(args),
+        out_specs=VMEM,
         out_shape=jax.ShapeDtypeStruct((8, W), f32),
-        scratch_shapes=corr_scratch(P_SIZE),
-        name="cross_corr",
-    )(centers, centers, *tables)
-
-
-def edge_offsets(sides, strips, received, tables):
-    return pl.pallas_call(
-        edge_kernel,
-        grid_spec=pltpu.PrefetchScalarGridSpec(
-            num_scalar_prefetch=1,
-            grid=(4, 2),
-            in_specs=[
-                pl.BlockSpec(
-                    (1, 1, 1, 1, HALF, W, W),
-                    lambda i, s, sides: (s, 0, 0, sides[i], sides[i] % 2, 0, 0),
-                )
-            ]
-            + [pl.BlockSpec(r.shape, lambda i, s, sides: (0, 0, 0, 0)) for r in received]
-            + [pl.BlockSpec(t.shape, lambda i, s, sides: (0, 0)) for t in tables],
-            out_specs=pl.BlockSpec((8, W), lambda i, s, sides: (0, 0)),
-            scratch_shapes=[pltpu.VMEM((HALF, W, W), bf16)] + corr_scratch(4 * P_SIZE),
-        ),
-        out_shape=jax.ShapeDtypeStruct((8, W), f32),
-        name="edge_corr",
-    )(sides, strips, *received, *tables)
+        scratch_shapes=[
+            pltpu.VMEM((P_SIZE // 2, 2, 2 * W, 2 * W), bf16),
+            pltpu.VMEM((P_SIZE // 2, 2, 2 * W, 2 * W), bf16),
+            pltpu.VMEM((P_SIZE, W), f32),
+            pltpu.VMEM((P_SIZE, W), f32),
+        ],
+        compiler_params=pltpu.CompilerParams(vmem_limit_bytes=CORR_VMEM),
+        name=name,
+    )(*args)
 
 
 def three_terms(values):
@@ -296,11 +251,11 @@
 
 def stiffness_rows(stiffness):
     row = lax.broadcasted_iota(jnp.int32, (32, W), 0)
-    return jnp.where((row // 8) % 2 == 0, stiffness[0], stiffness[1])
-
-
-def sided(parity, messages):
-    even_x, even_y = parity[0] == 0, parity[1] == 0
+    return jnp.where((row // 8) % 2 == 0, stiffness[0, 0, 0], stiffness[1, 0, 0])
+
+
+def sided(messages):
+    even_x, even_y = lax.rem(lax.axis_index("tx"), 2) == 0, lax.rem(lax.axis_index("ty"), 2) == 0
     p1, p2, p3, p4 = (m[0:2, :] for m in messages)
     east, west = jnp.where(even_x, p1, p2), jnp.where(even_x, p2, p1)
     south, north = jnp.where(even_y, p3, p4), jnp.where(even_y, p4, p3)
@@ -333,46 +288,63 @@
     return jnp.concatenate([rows, jnp.zeros((6, W), f32)], 0)
 
 
-def start_kernel(parity, stiffness, slots, valid, cross, edge, m1, m2, m3, m4, field_ref, vals_ref, shift_ref, inv_ref):
+def prepare_kernel(stiffness, counts, lists, slots_ref, valid_ref, inv_ref):
+    slots_ref[...] = jnp.zeros((8, W), jnp.int32)
+    lane = lax.broadcasted_iota(jnp.int32, (8, W), 1)
+    used = jnp.zeros((8, W), jnp.int32)
+    for section in range(2):
+        for kind in range(5):
+            place = section * SLOTS + kind * P_SIZE
+            slots_ref[0:1, place : place + P_SIZE] = lists[section, 0, 0, kind, 0:1, :]
+            here = (lane >= place) & (lane < place + P_SIZE)
+            used = jnp.where(here, place + counts[section, 0, 0, kind], used)
+    live = jnp.where(lane < used, 1.0, 0.0)
+    valid_ref[...] = live
+    hit, inside = slot_tables(slots_ref)
+    numbers = scatter((live[0:1], live[0:1]), hit, inside)
+    springs = stiffness_rows(stiffness) * neighbour_sum(jnp.ones((32, W), f32))
+    inv_ref[...] = 1.0 / (anchor_weight + springs + numbers)
+
+
+def start_kernel(columns, rows, slots, valid, inverse, cross, e1, e2, e3, e4, m1, m2, m3, m4, field_ref, vals_ref, shift_ref):
     _, kind, slot = lane_kinds((2, W))
-    mirrored = to_partner(sided(parity, (m1, m2, m3, m4)))
+    mirrored = to_partner(sided((m1, m2, m3, m4)))
+    edge = e1[0:2, :] + e2[0:2, :] + e3[0:2, :] + e4[0:2, :]
     here = ((kind == 0) | (kind == 2)) == (slot < HALF)
-    shift = jnp.where(kind == 4, cross[0:2, :], jnp.where(here, edge[0:2, :], -mirrored))
+    shift = jnp.where(kind == 4, cross[0:2, :], jnp.where(here, edge, -mirrored))
+    tx, ty = lax.axis_index("tx"), lax.axis_index("ty")
+    closed = (kind == 0) & (tx == columns - 1) | (kind == 1) & (tx == 0)
+    closed = closed | (kind == 2) & (ty == rows - 1) | (kind == 3) & (ty == 0)
+    shift = jnp.where(closed, 0.0, shift)
     shift_ref[...] = padded(shift)
     hit, inside = slot_tables(slots)
     live = valid[0:1, :]
-    ones = jnp.ones((32, W), f32)
-    counts = scatter((live, live), hit, inside)
-    diagonal = anchor_weight + stiffness_rows(stiffness) * neighbour_sum(ones) + counts
-    inverse = 1.0 / diagonal
-    rhs = scatter((live * shift[0:1], live * shift[1:2]), hit, inside)
-    field = rhs / diagonal
+    field = scatter((live * shift[0:1], live * shift[1:2]), hit, inside) * inverse[...]
     field_ref[...] = field
-    inv_ref[...] = inverse
     vals_ref[...] = padded(jnp.concatenate(gather(field, hit, inside), 0))
 
 
-def advance(parity, stiffness, slots, valid, field, vals, messages, inverse):
+def advance(stiffness, slots, valid, field, vals, messages, inverse):
     hit, inside = slot_tables(slots)
     live = valid[0:1, :]
-    partner = partner_values(vals[0:2, :], sided(parity, messages)) * live
+    partner = partner_values(vals[0:2, :], sided(messages)) * live
     springs = stiffness_rows(stiffness)
     coupled = scatter((partner[0:1], partner[1:2]), hit, inside)
     result = (springs * neighbour_sum(field[...]) + coupled) * inverse[...]
     return result, jnp.concatenate(gather(result, hit, inside), 0), springs
 
 
-def step_kernel(parity, stiffness, slots, valid, inverse, field, vals, m1, m2, m3, m4, field_ref, vals_ref):
+def step_kernel(stiffness, slots, valid, inverse, field, vals, m1, m2, m3, m4, field_ref, vals_ref):
     result, found, _ = advance(
-        parity, stiffness, slots, valid, field, vals, (m1, m2, m3, m4), inverse
+        stiffness, slots, valid, field, vals, (m1, m2, m3, m4), inverse
     )
     field_ref[...] = result
     vals_ref[...] = padded(found)
 
 
-def moments_kernel(parity, stiffness, slots, valid, inverse, first, field, vals, m1, m2, m3, m4, field_ref, send_ref):
+def moments_kernel(stiffness, slots, valid, inverse, first, field, vals, m1, m2, m3, m4, field_ref, send_ref):
     third, found, springs = advance(
-        parity, stiffness, slots, valid, field, vals, (m1, m2, m3, m4), inverse
+        stiffness, slots, valid, field, vals, (m1, m2, m3, m4), inverse
     )
     field_ref[...] = third
     w0, w1 = first[...], field[...]
@@ -461,22 +433,15 @@
     out_ref[...] = solution[0] * first[...] + solution[1] * second[...] + solution[2] * third[...]
 
 
-SMEM = pl.BlockSpec(memory_space=pltpu.SMEM)
-VMEM = pl.BlockSpec(memory_space=pltpu.VMEM)
-
-
 def shaped(*shapes):
     return [jax.ShapeDtypeStruct(s, f32) for s in shapes]
 
 
 def local(columns, rows, strips, centers, match_lists, match_counts, spring_stiffness):
     tables = [jnp.asarray(t) for t in fourier_tables()]
-    parity_x, parity_y = lax.axis_index("tx") % 2, lax.axis_index("ty") % 2
-    parity = jnp.stack([parity_x, parity_y]).astype(jnp.int32)
-    sides = jnp.stack([parity_x, 1 - parity_x, 2 + parity_y, 3 - parity_y]).astype(jnp.int32)
 
     def swaps(count, odd):
-        pairs = [(i, i + 1) for i in range(odd, count - 1, 2)]
+        pairs = [(i, (i + 1) % count) for i in range(odd, count, 2)]
         return pairs + [(b, a) for a, b in pairs]
 
     routes = [
@@ -486,60 +451,70 @@
         ("ty", swaps(rows, 1)),
     ]
 
-    def exchange(arrays):
-        return [lax.ppermute(a, axis, route) for a, (axis, route) in zip(arrays, routes)]
-
-    outgoing = []
+    def exchange(array, number):
+        return lax.ppermute(array, *routes[number])
+
+    received = []
     for number in range(4):
-        side = sides[number]
+        side = side_of(number)
         piece = lax.dynamic_slice(
             strips,
-            (0, 0, 0, side, (1 - side % 2) * HALF, 0, 0),
+            (0, 0, 0, side, (1 - lax.rem(side, 2)) * HALF, 0, 0),
             (2, 1, 1, 1, HALF, W, W),
         )
-        outgoing.append(piece.reshape(2, HALF, W, W))
-    received = exchange(outgoing)
-    cross = cross_offsets(centers, tables)
-    edge = edge_offsets(sides, strips, received, tables)
-
-    def on_lanes(values):
-        return jnp.pad(values.reshape(1, 2 * SLOTS), ((0, 7), (0, W - 2 * SLOTS)))
-
-    slots = on_lanes(match_lists[..., 0])
-    live = jnp.arange(P_SIZE, dtype=jnp.int32) < match_counts[..., None]
-    valid = on_lanes(live.astype(f32))
-    stiffness = spring_stiffness.reshape(2)
-
-    messages = exchange([edge] * 4)
-    first, vals, shift, inverse = pl.pallas_call(
-        start_kernel,
-        in_specs=[SMEM, SMEM] + [VMEM] * 8,
-        out_specs=[VMEM] * 4,
-        out_shape=shaped((32, W), (8, W), (8, W), (32, W)),
+        received.append(exchange(piece.reshape(2, HALF, W, W), number))
+    slots, valid, inverse = pl.pallas_call(
+        prepare_kernel,
+        in_specs=[SMEM, SMEM, VMEM],
+        out_specs=[VMEM] * 3,
+        out_shape=[jax.ShapeDtypeStruct((8, W), jnp.int32)] + shaped((8, W), (32, W)),
+        compiler_params=SMALL,
+        name="prepare",
+    )(spring_stiffness, match_counts, jnp.swapaxes(match_lists, 4, 5))
+    edges, messages = [None] * 4, [None] * 4
+    for number in (2, 3, 0, 1):
+        edges[number] = corr_call(
+            functools.partial(edge_kernel, number),
+            f"edge_{number}",
+            strips,
+            received[number],
+            *tables,
+        )
+        messages[number] = exchange(edges[number], number)
+    cross = corr_call(cross_kernel, "cross", centers, *tables)
+    first, vals, shift = pl.pallas_call(
+        functools.partial(start_kernel, columns, rows),
+        in_specs=[VMEM] * 12,
+        out_specs=[VMEM] * 3,
+        out_shape=shaped((32, W), (8, W), (8, W)),
+        compiler_params=SMALL,
         name="start",
-    )(parity, stiffness, slots, valid, cross, edge, *messages)
-    messages = exchange([vals] * 4)
+    )(slots, valid, inverse, cross, *edges, *messages)
+    messages = [exchange(vals, number) for number in range(4)]
     second, vals = pl.pallas_call(
         step_kernel,
-        in_specs=[SMEM, SMEM] + [VMEM] * 9,
+        in_specs=[SMEM] + [VMEM] * 9,
         out_specs=[VMEM] * 2,
         out_shape=shaped((32, W), (8, W)),
+        compiler_params=SMALL,
         name="step",
-    )(parity, stiffness, slots, valid, inverse, first, vals, *messages)
-    messages = exchange([vals] * 4)
+    )(spring_stiffness, slots, valid, inverse, first, vals, *messages)
+    messages = [exchange(vals, number) for number in range(4)]
     third, sent = pl.pallas_call(
         moments_kernel,
-        in_specs=[SMEM, SMEM] + [VMEM] * 10,
+        in_specs=[SMEM] + [VMEM] * 10,
         out_specs=[VMEM] * 2,
         out_shape=shaped((32, W), (2 * rows * columns, W)),
+        compiler_params=SMALL,
         name="moments",
-    )(parity, stiffness, slots, valid, inverse, first, second, vals, *messages)
+    )(spring_stiffness, slots, valid, inverse, first, second, vals, *messages)
     gathered = lax.all_to_all(sent, ("ty", "tx"), 0, 0, tiled=True)
     solution = pl.pallas_call(
         functools.partial(finish_kernel, columns),
         in_specs=[VMEM] * 4,
         out_specs=VMEM,
         out_shape=jax.ShapeDtypeStruct((32, W), f32),
+        compiler_params=SMALL,
         name="finish",
     )(gathered, first, second, third)
     vertex_shift = solution.reshape(2, 2, 1, 1, V * V)

time: 100 us -> 69.6 us (0.70)
  Pallas kernels: 30.4 us -> 14 us
  starting transfers between devices: 46.4 us -> 31 us
  waiting for transfers between devices: 13.4 us -> 17.5 us
  other arithmetic: 1.95 us -> 0 us
    pallas_call x5 -> x9, Pallas kernels: 28.6 us -> 13.2 us  [the longest x5 9.42 us: corr_call(): pl.pallas_call(kernel, in_specs=[VMEM] * len(args), out_specs=VMEM, out_s...]
    all_to_all x1, starting transfers between devices: 13.9 us -> 5.91 us  [local(): gathered = lax.all_to_all(sent, ('ty', 'tx'), 0, 0, tiled=True)]
    ppermute x16, starting transfers between devices: 32.5 us -> 25.1 us  [exchange(): return lax.ppermute(array, *routes[number])]
    ppermute x16, waiting for transfers between devices: 4.69 us -> 8.13 us  [exchange(): return lax.ppermute(array, *routes[number])]
    another operation x2 -> x0, other arithmetic: 1.27 us -> none  [the longest x1 0.66 us: local(): jnp.stack([parity_x, 1 - parity_x, 2 + parity_y, 3 - parity_y])]
    unnamed x38 -> x31, local copies, waits for them, and re-layouts: 3.11 us -> 3.74 us
  transfers between devices with their start and end apart: 17 -> 17, of which waited for: 4 -> 6; matrix products, arithmetic and copies ran while one was open for 4% -> 1% of each run, Pallas kernels for 6% -> 15%
where the time goes in v2:
time: 69.6 us; the launch traced here: 69.3 us
  starting transfers between devices  31 us (45%)
  waiting for transfers between devices  17.5 us (25%)
  Pallas kernels  14 us (20%)
  local copies, waits for them, and re-layouts  5.87 us (8%)
  between operations  0.89 us (1%)
    ppermute x16, starting transfers between devices, exchange(): return lax.ppermute(array, *routes[number])  25.1 us
    pallas_call x5, Pallas kernels, corr_call(): pl.pallas_call(kernel, in_specs=[VMEM] * len(args), out_specs=VMEM, out_s...  9.42 us
    all_to_all x1, waiting for transfers between devices, local(): gathered = lax.all_to_all(sent, ('ty', 'tx'), 0, 0, tiled=True)  9.36 us
    ppermute x16, waiting for transfers between devices, exchange(): return lax.ppermute(array, *routes[number])  8.13 us
    all_to_all x1, starting transfers between devices, local(): gathered = lax.all_to_all(sent, ('ty', 'tx'), 0, 0, tiled=True)  5.91 us
    unnamed x31, local copies, waits for them, and re-layouts  3.74 us
    pallas_call x1, Pallas kernels, local(): pl.pallas_call(moments_kernel, in_specs=[SMEM] + [VMEM] * 10, out_specs=[...  1.73 us
    reshape x1, local copies, waits for them, and re-layouts, local(): received.append(exchange(piece.reshape(2, HALF, W, W), number))  1.44 us
  transfers between devices with their start and end apart: 17, of which 6 were waited for; matrix products, arithmetic and copies ran while one was open for 1% of the time, Pallas kernels for 15%

profile of v2, /device:TPU:1, one launch (start us, length us, event | category | flops | bytes accessed | tf_op | source)
XLA Modules:
  0.0 69.3 jit_solution(17267821118121802012)
XLA Ops:
  0.6 0.0 copy-start.3
  0.6 0.0 copy-start.11
  0.7 0.0 copy-start
  0.7 1.4 %dynamic-slice_bitcast_fusion = (bf16[2,4,128,128]{3,2,1,0:T(8,128)(2,1)S(1)}, bf16[2,4,128,128]{3,2,1,0:T(8,128)(2,1)S(1)}, bf16[2,4,128,128]{3,2,1,0:T(8,128)(2,1)S(1)}, bf16[2,4,128,128]{3,2,1,0:T(8,128)(2,1)S(1)}) fusion(bf16[2,1,1,4,8,128,128]{6,5,4,3,2,1,0:T(8,128)(2,1)} %strips.7, s32[]{:T(128)S(6)} %select_n.30, s32[]{:T(128)S(6)} %select_n.31, ...), kind=kLoop, calls=%fused_computation | loop fusion | bytes 2097184 | tf_op jit(solution)/shard_map/reshape | solution.py:465
  2.1 2.1 %collective-permute-start = (bf16[2,4,128,128]{3,2,1,0:T(8,128)(2,1)S(1)}, bf16[2,4,128,128]{3,2,1,0:T(8,128)(2,1)S(1)}, u32[]{:S(2)}, u32[]{:S(2)}) collective-permute-start(bf16[2,4,128,128]{3,2,1,0:T(8,128)(2,1)S(1)} %get-tuple-element.29), channel_id=1, source_target_pairs={{0,1},{2,3},{4,5},{6,7},{8,9},{10,11},{12,13},{14,15},{1,0},{3,2},... | collective-permute-start | bytes 786440 | tf_op jit(solution)/shard_map/ppermute | solution.py:455
  4.3 4.3 %collective-permute-start.1 = (bf16[2,4,128,128]{3,2,1,0:T(8,128)(2,1)S(1)}, bf16[2,4,128,128]{3,2,1,0:T(8,128)(2,1)S(1)}, u32[]{:S(2)}, u32[]{:S(2)}) collective-permute-start(bf16[2,4,128,128]{3,2,1,0:T(8,128)(2,1)S(1)} %get-tuple-element.28), channel_id=1, source_target_pairs={{1,2},{3,4},{5,6},{7,8},{9,10},{11,12},{13,14},{15,0},{2,1},{4,3},... | collective-permute-start | bytes 786440 | tf_op jit(solution)/shard_map/ppermute | solution.py:455
  8.5 1.2 %collective-permute-start.2 = (bf16[2,4,128,128]{3,2,1,0:T(8,128)(2,1)S(1)}, bf16[2,4,128,128]{3,2,1,0:T(8,128)(2,1)S(1)}, u32[]{:S(2)}, u32[]{:S(2)}) collective-permute-start(bf16[2,4,128,128]{3,2,1,0:T(8,128)(2,1)S(1)} %get-tuple-element.27), channel_id=1, source_target_pairs={{0,16},{32,48},{64,80},{96,112},{16,0},{48,32},{80,64},{112,96},{1... | collective-permute-start | bytes 786440 | tf_op jit(solution)/shard_map/ppermute | solution.py:455
  9.8 1.5 %collective-permute-start.3 = (bf16[2,4,128,128]{3,2,1,0:T(8,128)(2,1)S(1)}, bf16[2,4,128,128]{3,2,1,0:T(8,128)(2,1)S(1)}, u32[]{:S(2)}, u32[]{:S(2)}) collective-permute-start(bf16[2,4,128,128]{3,2,1,0:T(8,128)(2,1)S(1)} %get-tuple-element.26), channel_id=1, source_target_pairs={{16,32},{48,64},{80,96},{112,0},{32,16},{64,48},{96,80},{0,112},{1... | collective-permute-start | bytes 786440 | tf_op jit(solution)/shard_map/ppermute | solution.py:455
  11.3 0.0 collective-permute-done.received
  11.3 0.0 copy-done.3
  11.3 0.0 copy-done.11
  11.3 0.0 copy-done
  11.3 0.0 copy-start.1
  11.3 0.9 %copy-done.1 = bf16[512,256]{1,0:T(8,128)(2,1)S(1)} copy-done((bf16[512,256]{1,0:T(8,128)(2,1)S(1)}, bf16[512,256]{1,0:T(8,128)(2,1)}, u32[]{:S(2)}) %copy-start.1) | copy-done | bytes 262168
  12.3 0.9 %copy-done.4 = bf16[256,256]{1,0:T(8,128)(2,1)S(1)} copy-done((bf16[256,256]{1,0:T(8,128)(2,1)S(1)}, bf16[256,256]{1,0:T(8,128)(2,1)}, u32[]{:S(2)}) %copy-start.4) | copy-done | bytes 131096
  13.2 0.9 %copy-done.6 = bf16[128,384]{1,0:T(8,128)(2,1)S(1)} copy-done((bf16[128,384]{1,0:T(8,128)(2,1)S(1)}, bf16[128,384]{1,0:T(8,128)(2,1)}, u32[]{:S(2)}) %copy-start.6) | copy-done | bytes 98328
  14.1 0.8 %copy-done.8 = f32[128,128]{1,0:T(8,128)S(1)} copy-done((f32[128,128]{1,0:T(8,128)S(1)}, f32[128,128]{1,0:T(8,128)}, u32[]{:S(2)}) %copy-start.8) | copy-done | bytes 65560
  14.9 1.9 %edge_0.1.e1 = f32[8,128]{1,0:T(8,128)S(1)} custom-call(bf16[2,1,1,4,8,128,128]{6,5,4,3,2,1,0:T(8,128)(2,1)S(1)} %copy-done, bf16[2,4,128,128]{3,2,1,0:T(8,128)(2,1)S(1)} %collective-permute-done.received, bf16[256,256]{1,0:T(8,128)(2,1)S(1)} %copy-done.4, bf16[288,256]{1,0:T(8,128)(2,1)S(1)} %copy-done.3, bf16[512,256]{1,0:T(8,128)(2,1)S(1)} %copy-done.1, ...), custom_call_target="tpu_custom_call" | custom-call | tf_op jit(solution)/shard_map/edge_0/pallas_call | solution.py:187
  16.8 0.2 collective-permute-start.4
  17.0 0.0 collective-permute-done.1.received
  17.0 1.9 %edge_1.1.e2 = f32[8,128]{1,0:T(8,128)S(1)} custom-call(bf16[2,1,1,4,8,128,128]{6,5,4,3,2,1,0:T(8,128)(2,1)S(1)} %copy-done, bf16[2,4,128,128]{3,2,1,0:T(8,128)(2,1)S(1)} %collective-permute-done.1.received, bf16[256,256]{1,0:T(8,128)(2,1)S(1)} %copy-done.4, bf16[288,256]{1,0:T(8,128)(2,1)S(1)} %copy-done.3, bf16[512,256]{1,0:T(8,128)(2,1)S(1)} %copy-done.1, ...), custom_call_target="tpu_custom_call" | custom-call | tf_op jit(solution)/shard_map/edge_1/pallas_call | solution.py:187
  18.9 4.3 %collective-permute-start.5 = (f32[8,128]{1,0:T(8,128)S(1)}, f32[8,128]{1,0:T(8,128)S(1)}, u32[]{:S(2)}, u32[]{:S(2)}) collective-permute-start(f32[8,128]{1,0:T(8,128)S(1)} %edge_1.1.e2), channel_id=1, source_target_pairs={{1,2},{3,4},{5,6},{7,8},{9,10},{11,12},{13,14},{15,0},{2,1},{4,3},... | collective-permute-start | bytes 12296 | tf_op jit(solution)/shard_map/ppermute | solution.py:455
  23.2 0.0 collective-permute-done.2.received
  23.2 1.9 %edge_2.1.e3 = f32[8,128]{1,0:T(8,128)S(1)} custom-call(bf16[2,1,1,4,8,128,128]{6,5,4,3,2,1,0:T(8,128)(2,1)S(1)} %copy-done, bf16[2,4,128,128]{3,2,1,0:T(8,128)(2,1)S(1)} %collective-permute-done.2.received, bf16[256,256]{1,0:T(8,128)(2,1)S(1)} %copy-done.4, bf16[288,256]{1,0:T(8,128)(2,1)S(1)} %copy-done.3, bf16[512,256]{1,0:T(8,128)(2,1)S(1)} %copy-done.1, ...), custom_call_target="tpu_custom_call" | custom-call | tf_op jit(solution)/shard_map/edge_2/pallas_call | solution.py:187
  25.1 0.0 copy-start.2
  25.1 0.0 copy-start.7
  25.1 0.0 copy-start.9
  25.1 0.0 copy-start.10
  25.2 0.0 copy-start.12
  25.2 0.0 copy-start.13
  25.2 2.2 %collective-permute-start.6 = (f32[8,128]{1,0:T(8,128)S(1)}, f32[8,128]{1,0:T(8,128)S(1)}, u32[]{:S(2)}, u32[]{:S(2)}) collective-permute-start(f32[8,128]{1,0:T(8,128)S(1)} %edge_2.1.e3), channel_id=1, source_target_pairs={{0,16},{32,48},{64,80},{96,112},{16,0},{48,32},{80,64},{112,96},{1... | collective-permute-start | bytes 12296 | tf_op jit(solution)/shard_map/ppermute | solution.py:455
  27.4 0.0 collective-permute-done.3.received
  27.4 1.9 %edge_3.1.e4 = f32[8,128]{1,0:T(8,128)S(1)} custom-call(bf16[2,1,1,4,8,128,128]{6,5,4,3,2,1,0:T(8,128)(2,1)S(1)} %copy-done, bf16[2,4,128,128]{3,2,1,0:T(8,128)(2,1)S(1)} %collective-permute-done.3.received, bf16[256,256]{1,0:T(8,128)(2,1)S(1)} %copy-done.5, bf16[288,256]{1,0:T(8,128)(2,1)S(1)} %copy-done.3, bf16[512,256]{1,0:T(8,128)(2,1)S(1)} %copy-done.1, ...), custom_call_target="tpu_custom_call" | custom-call | tf_op jit(solution)/shard_map/edge_3/pallas_call | solution.py:187
  29.2 1.6 %collective-permute-start.7 = (f32[8,128]{1,0:T(8,128)S(1)}, f32[8,128]{1,0:T(8,128)S(1)}, u32[]{:S(2)}, u32[]{:S(2)}) collective-permute-start(f32[8,128]{1,0:T(8,128)S(1)} %edge_3.1.e4), channel_id=1, source_target_pairs={{16,32},{48,64},{80,96},{112,0},{32,16},{64,48},{96,80},{0,112},{1... | collective-permute-start | bytes 12296 | tf_op jit(solution)/shard_map/ppermute | solution.py:455
  30.9 0.1 copy.20.stiffness
  31.0 1.9 %cross.1 = f32[8,128]{1,0:T(8,128)S(1)} custom-call(bf16[2,1,1,8,128,128]{5,4,3,2,1,0:T(8,128)(2,1)S(1)} %copy-done.10, bf16[256,256]{1,0:T(8,128)(2,1)S(1)} %copy-done.5, bf16[288,256]{1,0:T(8,128)(2,1)S(1)} %copy-done.3, bf16[512,256]{1,0:T(8,128)(2,1)S(1)} %copy-done.2, bf16[128,384]{1,0:T(8,128)(2,1)S(1)} %copy-done.7, f32[128,128]{1,0:T(8,128)S(1)} %copy-done.9, ...), custom_call_target="tpu_custom_call" | custom-call | tf_op jit(solution)/shard_map/cross/pallas_call | solution.py:187
  32.9 0.8 %prepare.1 = (s32[8,128]{1,0:T(8,128)S(1)}, f32[8,128]{1,0:T(8,128)S(1)}, f32[32,128]{1,0:T(8,128)S(1)}) custom-call(f32[2,1,1]{2,1,0:T(1,128)S(1)} %copy.20.stiffness, s32[2,1,1,5]{3,2,1,0:T(1,128)S(1)} %copy-done.13, s32[2,1,1,5,2,8]{5,4,3,2,1,0:T(2,128)S(1)} %bitcast.13), custom_call_target="tpu_custom_call" | custom-call | tf_op jit(solution)/shard_map/prepare/pallas_call | solution.py:466
  33.7 0.0 collective-permute-done.4.m1
  33.7 0.0 collective-permute-done.5.m2
  33.8 0.0 collective-permute-done.6.m3
  33.8 0.0 collective-permute-done.7.m4
  33.8 0.4 start.1
  34.1 2.7 %collective-permute-start.10 = (f32[8,128]{1,0:T(8,128)S(1)}, f32[8,128]{1,0:T(8,128)S(1)}, u32[]{:S(2)}, u32[]{:S(2)}) collective-permute-start(f32[8,128]{1,0:T(8,128)S(1)} %get-tuple-element.16.vals), channel_id=1, source_target_pairs={{0,16},{32,48},{64,80},{96,112},{16,0},{48,32},{80,64},{112,96},{1... | collective-permute-start | bytes 12296 | tf_op jit(solution)/shard_map/ppermute | solution.py:455
  36.8 0.0 collective-permute-start.11
  36.8 0.0 collective-permute-start.8
  36.8 0.7 collective-permute-start.9
  37.5 0.2 collective-permute-done.10.m3
  37.7 2.2 %collective-permute-done.11.m4 = f32[8,128]{1,0:T(8,128)S(1)} collective-permute-done((f32[8,128]{1,0:T(8,128)S(1)}, f32[8,128]{1,0:T(8,128)S(1)}, u32[]{:S(2)}, u32[]{:S(2)}) %collective-permute-start.11) | collective-permute-done | bytes 4128 | tf_op jit(solution)/shard_map/ppermute | solution.py:455
  39.9 0.0 collective-permute-done.8.m1
  39.9 2.7 %collective-permute-done.9.m2 = f32[8,128]{1,0:T(8,128)S(1)} collective-permute-done((f32[8,128]{1,0:T(8,128)S(1)}, f32[8,128]{1,0:T(8,128)S(1)}, u32[]{:S(2)}, u32[]{:S(2)}) %collective-permute-start.9) | collective-permute-done | bytes 4128 | tf_op jit(solution)/shard_map/ppermute | solution.py:455
  42.6 0.9 %step.1 = (f32[32,128]{1,0:T(8,128)S(1)}, f32[8,128]{1,0:T(8,128)S(1)}) custom-call(f32[2,1,1]{2,1,0:T(1,128)S(1)} %copy.20.stiffness, s32[8,128]{1,0:T(8,128)S(1)} %get-tuple-element.12.slots, f32[8,128]{1,0:T(8,128)S(1)} %get-tuple-element.13.valid, f32[32,128]{1,0:T(8,128)S(1)} %get-tuple-element.14.inverse, f32[32,128]{1,0:T(8,128)S(1)} %get-tuple-element.15.field.first, ...), custom_call_target="tpu_custom_call" | custom-call | tf_op jit(solution)/shard_map/step/pallas_call | solution.py:494
  43.5 0.1 collective-permute-start.12
  43.6 0.7 %collective-permute-start.13 = (f32[8,128]{1,0:T(8,128)S(1)}, f32[8,128]{1,0:T(8,128)S(1)}, u32[]{:S(2)}, u32[]{:S(2)}) collective-permute-start(f32[8,128]{1,0:T(8,128)S(1)} %get-tuple-element.18.vals), channel_id=1, source_target_pairs={{1,2},{3,4},{5,6},{7,8},{9,10},{11,12},{13,14},{15,0},{2,1},{4,3},... | collective-permute-start | bytes 12296 | tf_op jit(solution)/shard_map/ppermute | solution.py:455
  44.4 3.1 %collective-permute-start.14 = (f32[8,128]{1,0:T(8,128)S(1)}, f32[8,128]{1,0:T(8,128)S(1)}, u32[]{:S(2)}, u32[]{:S(2)}) collective-permute-start(f32[8,128]{1,0:T(8,128)S(1)} %get-tuple-element.18.vals), channel_id=1, source_target_pairs={{0,16},{32,48},{64,80},{96,112},{16,0},{48,32},{80,64},{112,96},{1... | collective-permute-start | bytes 12296 | tf_op jit(solution)/shard_map/ppermute | solution.py:455
  47.5 0.3 collective-permute-start.15
  47.8 0.0 collective-permute-done.12.m1
  47.8 1.7 %collective-permute-done.13.m2 = f32[8,128]{1,0:T(8,128)S(1)} collective-permute-done((f32[8,128]{1,0:T(8,128)S(1)}, f32[8,128]{1,0:T(8,128)S(1)}, u32[]{:S(2)}, u32[]{:S(2)}) %collective-permute-start.13) | collective-permute-done | bytes 4128 | tf_op jit(solution)/shard_map/ppermute | solution.py:455
  49.5 0.0 collective-permute-done.14.m3
  49.5 1.3 %collective-permute-done.15.m4 = f32[8,128]{1,0:T(8,128)S(1)} collective-permute-done((f32[8,128]{1,0:T(8,128)S(1)}, f32[8,128]{1,0:T(8,128)S(1)}, u32[]{:S(2)}, u32[]{:S(2)}) %collective-permute-start.15) | collective-permute-done | bytes 4128 | tf_op jit(solution)/shard_map/ppermute | solution.py:455
  50.8 1.7 %moments.1 = (f32[32,128]{1,0:T(8,128)S(1)}, f32[256,128]{1,0:T(8,128)}) custom-call(f32[2,1,1]{2,1,0:T(1,128)S(1)} %copy.20.stiffness, s32[8,128]{1,0:T(8,128)S(1)} %get-tuple-element.12.slots, f32[8,128]{1,0:T(8,128)S(1)} %get-tuple-element.13.valid, f32[32,128]{1,0:T(8,128)S(1)} %get-tuple-element.14.inverse, ...), custom_call_target="tpu_custom_call" | custom-call | tf_op jit(solution)/shard_map/moments/pallas_call | solution.py:503
  52.5 5.9 %all-to-all-start = ((f32[128,2,128]{2,1,0:T(2,128)}), f32[128,2,128]{2,1,0:T(2,128)S(1)}, u32[]{:S(2)}, u32[]{:S(2)}) async-start(f32[128,2,128]{2,1,0:T(2,128)} %bitcast.5), calls=%async_computation | async-start | bytes 262144 | tf_op jit(solution)/shard_map/all_to_all | solution.py:511
  58.5 0.7 reshape.30
  59.2 9.4 %all-to-all-done = f32[128,2,128]{2,1,0:T(2,128)S(1)} async-done(((f32[128,2,128]{2,1,0:T(2,128)}), f32[128,2,128]{2,1,0:T(2,128)S(1)}, u32[]{:S(2)}, u32[]{:S(2)}) %all-to-all-start) | async-done | bytes 131104 | tf_op jit(solution)/shard_map/all_to_all | solution.py:511
  68.5 0.8 %finish.1 = f32[32,128]{1,0:T(8,128)} custom-call(f32[256,128]{1,0:T(8,128)S(1)} %bitcast.12, f32[32,128]{1,0:T(8,128)S(1)} %get-tuple-element.15.field.first, f32[32,128]{1,0:T(8,128)S(1)} %get-tuple-element.17.field.second, f32[32,128]{1,0:T(8,128)S(1)} %get-tuple-element.20.third), custom_call_target="tpu_custom_call" | custom-call | tf_op jit(solution)/shard_map/finish/pallas_call | solution.py:512
  (14 shorter events, 0.0 us)
Async XLA Ops:
  0.6 10.7 %copy-start.3 = (bf16[288,256]{1,0:T(8,128)(2,1)S(1)}, bf16[288,256]{1,0:T(8,128)(2,1)}, u32[]{:S(2)}) copy-start(bf16[288,256]{1,0:T(8,128)(2,1)} %constant.53.clone.t2) | copy-start | bytes 442372
  0.6 10.7 %copy-start.11 = (f32[8,128]{1,0:T(8,128)S(1)}, f32[8,128]{1,0:T(8,128)}, u32[]{:S(2)}) copy-start(f32[8,128]{1,0:T(8,128)} %constant.57.clone.lag_cols) | copy-start | bytes 12292
  0.7 10.6 %copy-start = (bf16[2,1,1,4,8,128,128]{6,5,4,3,2,1,0:T(8,128)(2,1)S(1)}, bf16[2,1,1,4,8,128,128]{6,5,4,3,2,1,0:T(8,128)(2,1)}, u32[]{:S(2)}) copy-start(bf16[2,1,1,4,8,128,128]{6,5,4,3,2,1,0:T(8,128)(2,1)} %strips.7) | copy-start | bytes 6291460
  2.1 9.1 %collective-permute-start = (bf16[2,4,128,128]{3,2,1,0:T(8,128)(2,1)S(1)}, bf16[2,4,128,128]{3,2,1,0:T(8,128)(2,1)S(1)}, u32[]{:S(2)}, u32[]{:S(2)}) collective-permute-start(bf16[2,4,128,128]{3,2,1,0:T(8,128)(2,1)S(1)} %get-tuple-element.29), channel_id=1, source_target_pairs={{0,1},{2,3},{4,5},{6,7},{8,9},{10,11},{12,13},{14,15},{1,0},{3,2},... | collective-permute-start | bytes 786440 | tf_op jit(solution)/shard_map/ppermute | solution.py:455
  4.3 12.7 %collective-permute-start.1 = (bf16[2,4,128,128]{3,2,1,0:T(8,128)(2,1)S(1)}, bf16[2,4,128,128]{3,2,1,0:T(8,128)(2,1)S(1)}, u32[]{:S(2)}, u32[]{:S(2)}) collective-permute-start(bf16[2,4,128,128]{3,2,1,0:T(8,128)(2,1)S(1)} %get-tuple-element.28), channel_id=1, source_target_pairs={{1,2},{3,4},{5,6},{7,8},{9,10},{11,12},{13,14},{15,0},{2,1},{4,3},... | collective-permute-start | bytes 786440 | tf_op jit(solution)/shard_map/ppermute | solution.py:455
  8.5 14.7 %collective-permute-start.2 = (bf16[2,4,128,128]{3,2,1,0:T(8,128)(2,1)S(1)}, bf16[2,4,128,128]{3,2,1,0:T(8,128)(2,1)S(1)}, u32[]{:S(2)}, u32[]{:S(2)}) collective-permute-start(bf16[2,4,128,128]{3,2,1,0:T(8,128)(2,1)S(1)} %get-tuple-element.27), channel_id=1, source_target_pairs={{0,16},{32,48},{64,80},{96,112},{16,0},{48,32},{80,64},{112,96},{1... | collective-permute-start | bytes 786440 | tf_op jit(solution)/shard_map/ppermute | solution.py:455
  9.8 17.6 %collective-permute-start.3 = (bf16[2,4,128,128]{3,2,1,0:T(8,128)(2,1)S(1)}, bf16[2,4,128,128]{3,2,1,0:T(8,128)(2,1)S(1)}, u32[]{:S(2)}, u32[]{:S(2)}) collective-permute-start(bf16[2,4,128,128]{3,2,1,0:T(8,128)(2,1)S(1)} %get-tuple-element.26), channel_id=1, source_target_pairs={{16,32},{48,64},{80,96},{112,0},{32,16},{64,48},{96,80},{0,112},{1... | collective-permute-start | bytes 786440 | tf_op jit(solution)/shard_map/ppermute | solution.py:455
  11.3 1.0 %copy-start.1 = (bf16[512,256]{1,0:T(8,128)(2,1)S(1)}, bf16[512,256]{1,0:T(8,128)(2,1)}, u32[]{:S(2)}) copy-start(bf16[512,256]{1,0:T(8,128)(2,1)} %constant.54.clone.t3) | copy-start | bytes 786436
  12.3 0.9 %copy-start.4 = (bf16[256,256]{1,0:T(8,128)(2,1)S(1)}, bf16[256,256]{1,0:T(8,128)(2,1)}, u32[]{:S(2)}) copy-start(bf16[256,256]{1,0:T(8,128)(2,1)} %constant.52.clone.t1) | copy-start | bytes 393220
  13.2 0.9 %copy-start.6 = (bf16[128,384]{1,0:T(8,128)(2,1)S(1)}, bf16[128,384]{1,0:T(8,128)(2,1)}, u32[]{:S(2)}) copy-start(bf16[128,384]{1,0:T(8,128)(2,1)} %constant.55.clone.t4) | copy-start | bytes 294916
  14.1 0.8 %copy-start.8 = (f32[128,128]{1,0:T(8,128)S(1)}, f32[128,128]{1,0:T(8,128)}, u32[]{:S(2)}) copy-start(f32[128,128]{1,0:T(8,128)} %constant.56.clone.t5) | copy-start | bytes 196612
  16.8 17.0 %collective-permute-start.4 = (f32[8,128]{1,0:T(8,128)S(1)}, f32[8,128]{1,0:T(8,128)S(1)}, u32[]{:S(2)}, u32[]{:S(2)}) collective-permute-start(f32[8,128]{1,0:T(8,128)S(1)} %edge_0.1.e1), channel_id=1, source_target_pairs={{0,1},{2,3},{4,5},{6,7},{8,9},{10,11},{12,13},{14,15},{1,0},{3,2},... | collective-permute-start | bytes 12296 | tf_op jit(solution)/shard_map/ppermute | solution.py:455
  18.9 8.5 %copy-start.5 = (bf16[256,256]{1,0:T(8,128)(2,1)S(1)}, bf16[256,256]{1,0:T(8,128)(2,1)}, u32[]{:S(2)}) copy-start(bf16[256,256]{1,0:T(8,128)(2,1)} %constant.52.clone.t1) | copy-start | bytes 393220
  18.9 14.9 %collective-permute-start.5 = (f32[8,128]{1,0:T(8,128)S(1)}, f32[8,128]{1,0:T(8,128)S(1)}, u32[]{:S(2)}, u32[]{:S(2)}) collective-permute-start(f32[8,128]{1,0:T(8,128)S(1)} %edge_1.1.e2), channel_id=1, source_target_pairs={{1,2},{3,4},{5,6},{7,8},{9,10},{11,12},{13,14},{15,0},{2,1},{4,3},... | collective-permute-start | bytes 12296 | tf_op jit(solution)/shard_map/ppermute | solution.py:455
  25.1 5.8 %copy-start.14 = (f32[2,1,1]{0,2,1:T(1,128)S(1)}, f32[2,1,1]{0,2,1:T(1,128)}, u32[]{:S(2)}) copy-start(f32[2,1,1]{0,2,1:T(1,128)} %param.15) | copy-start | bytes 28
  25.1 5.9 %copy-start.2 = (bf16[512,256]{1,0:T(8,128)(2,1)S(1)}, bf16[512,256]{1,0:T(8,128)(2,1)}, u32[]{:S(2)}) copy-start(bf16[512,256]{1,0:T(8,128)(2,1)} %constant.54.clone.t3) | copy-start | bytes 786436
  25.1 5.8 %copy-start.7 = (bf16[128,384]{1,0:T(8,128)(2,1)S(1)}, bf16[128,384]{1,0:T(8,128)(2,1)}, u32[]{:S(2)}) copy-start(bf16[128,384]{1,0:T(8,128)(2,1)} %constant.55.clone.t4) | copy-start | bytes 294916
  25.1 5.8 %copy-start.9 = (f32[128,128]{1,0:T(8,128)S(1)}, f32[128,128]{1,0:T(8,128)}, u32[]{:S(2)}) copy-start(f32[128,128]{1,0:T(8,128)} %constant.56.clone.t5) | copy-start | bytes 196612
  25.1 5.8 %copy-start.10 = (bf16[2,1,1,8,128,128]{5,4,3,2,1,0:T(8,128)(2,1)S(1)}, bf16[2,1,1,8,128,128]{5,4,3,2,1,0:T(8,128)(2,1)}, u32[]{:S(2)}) copy-start(bf16[2,1,1,8,128,128]{5,4,3,2,1,0:T(8,128)(2,1)} %pixels.1) | copy-start | bytes 1572868
  25.2 7.8 %copy-start.12 = (s32[2,1,1,5,8,2]{4,5,3,2,1,0:T(2,128)S(1)}, s32[2,1,1,5,8,2]{4,5,3,2,1,0:T(2,128)}, u32[]{:S(2)}) copy-start(s32[2,1,1,5,8,2]{4,5,3,2,1,0:T(2,128)} %param.13) | copy-start | bytes 1924
  25.2 7.8 %copy-start.13 = (s32[2,1,1,5]{3,2,1,0:T(1,128)S(1)}, s32[2,1,1,5]{3,2,1,0:T(1,128)}, u32[]{:S(2)}) copy-start(s32[2,1,1,5]{3,2,1,0:T(1,128)} %counts.1) | copy-start | bytes 124
  25.2 8.6 %collective-permute-start.6 = (f32[8,128]{1,0:T(8,128)S(1)}, f32[8,128]{1,0:T(8,128)S(1)}, u32[]{:S(2)}, u32[]{:S(2)}) collective-permute-start(f32[8,128]{1,0:T(8,128)S(1)} %edge_2.1.e3), channel_id=1, source_target_pairs={{0,16},{32,48},{64,80},{96,112},{16,0},{48,32},{80,64},{112,96},{1... | collective-permute-start | bytes 12296 | tf_op jit(solution)/shard_map/ppermute | solution.py:455
  29.2 4.5 %collective-permute-start.7 = (f32[8,128]{1,0:T(8,128)S(1)}, f32[8,128]{1,0:T(8,128)S(1)}, u32[]{:S(2)}, u32[]{:S(2)}) collective-permute-start(f32[8,128]{1,0:T(8,128)S(1)} %edge_3.1.e4), channel_id=1, source_target_pairs={{16,32},{48,64},{80,96},{112,0},{32,16},{64,48},{96,80},{0,112},{1... | collective-permute-start | bytes 12296 | tf_op jit(solution)/shard_map/ppermute | solution.py:455
  34.1 3.5 %collective-permute-start.10 = (f32[8,128]{1,0:T(8,128)S(1)}, f32[8,128]{1,0:T(8,128)S(1)}, u32[]{:S(2)}, u32[]{:S(2)}) collective-permute-start(f32[8,128]{1,0:T(8,128)S(1)} %get-tuple-element.16.vals), channel_id=1, source_target_pairs={{0,16},{32,48},{64,80},{96,112},{16,0},{48,32},{80,64},{112,96},{1... | collective-permute-start | bytes 12296 | tf_op jit(solution)/shard_map/ppermute | solution.py:455
  36.8 3.0 %collective-permute-start.11 = (f32[8,128]{1,0:T(8,128)S(1)}, f32[8,128]{1,0:T(8,128)S(1)}, u32[]{:S(2)}, u32[]{:S(2)}) collective-permute-start(f32[8,128]{1,0:T(8,128)S(1)} %get-tuple-element.16.vals), channel_id=1, source_target_pairs={{16,32},{48,64},{80,96},{112,0},{32,16},{64,48},{96,80},{0,112},{1... | collective-permute-start | bytes 12296 | tf_op jit(solution)/shard_map/ppermute | solution.py:455
  36.8 3.0 %collective-permute-start.8 = (f32[8,128]{1,0:T(8,128)S(1)}, f32[8,128]{1,0:T(8,128)S(1)}, u32[]{:S(2)}, u32[]{:S(2)}) collective-permute-start(f32[8,128]{1,0:T(8,128)S(1)} %get-tuple-element.16.vals), channel_id=1, source_target_pairs={{0,1},{2,3},{4,5},{6,7},{8,9},{10,11},{12,13},{14,15},{1,0},{3,2},... | collective-permute-start | bytes 12296 | tf_op jit(solution)/shard_map/ppermute | solution.py:455
  36.8 5.8 %collective-permute-start.9 = (f32[8,128]{1,0:T(8,128)S(1)}, f32[8,128]{1,0:T(8,128)S(1)}, u32[]{:S(2)}, u32[]{:S(2)}) collective-permute-start(f32[8,128]{1,0:T(8,128)S(1)} %get-tuple-element.16.vals), channel_id=1, source_target_pairs={{1,2},{3,4},{5,6},{7,8},{9,10},{11,12},{13,14},{15,0},{2,1},{4,3},... | collective-permute-start | bytes 12296 | tf_op jit(solution)/shard_map/ppermute | solution.py:455
  43.5 4.3 %collective-permute-start.12 = (f32[8,128]{1,0:T(8,128)S(1)}, f32[8,128]{1,0:T(8,128)S(1)}, u32[]{:S(2)}, u32[]{:S(2)}) collective-permute-start(f32[8,128]{1,0:T(8,128)S(1)} %get-tuple-element.18.vals), channel_id=1, source_target_pairs={{0,1},{2,3},{4,5},{6,7},{8,9},{10,11},{12,13},{14,15},{1,0},{3,2},... | collective-permute-start | bytes 12296 | tf_op jit(solution)/shard_map/ppermute | solution.py:455
  43.6 5.9 %collective-permute-start.13 = (f32[8,128]{1,0:T(8,128)S(1)}, f32[8,128]{1,0:T(8,128)S(1)}, u32[]{:S(2)}, u32[]{:S(2)}) collective-permute-start(f32[8,128]{1,0:T(8,128)S(1)} %get-tuple-element.18.vals), channel_id=1, source_target_pairs={{1,2},{3,4},{5,6},{7,8},{9,10},{11,12},{13,14},{15,0},{2,1},{4,3},... | collective-permute-start | bytes 12296 | tf_op jit(solution)/shard_map/ppermute | solution.py:455
  44.4 5.1 %collective-permute-start.14 = (f32[8,128]{1,0:T(8,128)S(1)}, f32[8,128]{1,0:T(8,128)S(1)}, u32[]{:S(2)}, u32[]{:S(2)}) collective-permute-start(f32[8,128]{1,0:T(8,128)S(1)} %get-tuple-element.18.vals), channel_id=1, source_target_pairs={{0,16},{32,48},{64,80},{96,112},{16,0},{48,32},{80,64},{112,96},{1... | collective-permute-start | bytes 12296 | tf_op jit(solution)/shard_map/ppermute | solution.py:455
  47.5 3.3 %collective-permute-start.15 = (f32[8,128]{1,0:T(8,128)S(1)}, f32[8,128]{1,0:T(8,128)S(1)}, u32[]{:S(2)}, u32[]{:S(2)}) collective-permute-start(f32[8,128]{1,0:T(8,128)S(1)} %get-tuple-element.18.vals), channel_id=1, source_target_pairs={{16,32},{48,64},{80,96},{112,0},{32,16},{64,48},{96,80},{0,112},{1... | collective-permute-start | bytes 12296 | tf_op jit(solution)/shard_map/ppermute | solution.py:455
  52.5 16.0 %all-to-all-start = ((f32[128,2,128]{2,1,0:T(2,128)}), f32[128,2,128]{2,1,0:T(2,128)S(1)}, u32[]{:S(2)}, u32[]{:S(2)}) async-start(f32[128,2,128]{2,1,0:T(2,128)} %bitcast.5), calls=%async_computation | async-start | bytes 262144 | tf_op jit(solution)/shard_map/all_to_all | solution.py:511
